TPU v7x, 32 devices: a whole 2x2x4 slice. The times are simulated.
32 devices in a mesh: grow: 4 (over z), gy: 4 (over x, core), gz: 2 (over y).
Axes of the slice: x: 2, y: 2, z: 4, core: 2. Of those that a mesh axis runs over, the one named last changes fastest.
Arguments:
- labels: int32 [128, 32, 256], P('grow', 'gy', 'gz'), may hold values from 0 to 3
- potential: float32 [2, 128, 32, 256], P(None, 'grow', 'gy', 'gz'), may hold values from -3 to 3
- melt_codes: int32 [16, 32, 256], P(None, 'gy', 'gz'), may hold values from 0 to 7
- melt_table: float32 [2, 8], replicated, may hold values from -1 to 1
Outputs:
- phases: float32 [4, 128, 32, 256], P(None, 'grow', 'gy', 'gz')
- potentials: float32 [2, 128, 32, 256], P(None, 'grow', 'gy', 'gz')
All inputs are finite; a program needn't handle non-finite values.
Results may differ from a plain program's by a relative error of at most 0.0001.
Values sent between devices are 32-bit elements; how exact they have to be, the bound alone decides.
A program may use at most 64 MiB of HBM per device.

v0:
```python
import functools

import jax
import jax.numpy as jnp
from jax import lax
from jax.experimental import pallas as pl
from jax.experimental.pallas import tpu as pltpu
from jax.sharding import PartitionSpec as P

STEPS_BEFORE = 3
STEPS_AFTER = 2
STEPS = STEPS_BEFORE + STEPS_AFTER
HALF = 7
WIDE = 2 * HALF
MESH = pl.DeviceIdType.MESH


class Plan:
    def __init__(self, planes, rows, shift):
        self.planes, self.rows, self.shift = planes, rows, shift
        self.skip = (shift - STEPS) // 8 * 8
        self.own = planes - self.skip
        self.above = shift + STEPS
        self.upper = -(-self.above // 8) * 8
        self.deep = self.own + self.upper
        self.first = shift - self.skip
        self.start = self.first - STEPS + 1
        self.tiles = -(-(planes + 2 * (STEPS - 1)) // 8)
        self.tall = rows + 2 * STEPS
        self.slots = self.tall // 2


def gather_kernel(plan, mesh_shape, levels, lab, pot, codes, table, main, strip, pack, lab_up, pot_up, g_send, g_recv, y_send, y_recv, z_send, z_recv):
    g, y, z = lax.axis_index("grow"), lax.axis_index("gy"), lax.axis_index("gz")
    count_g, count_y, count_z = mesh_shape
    rows, own, tall = plan.rows, plan.own, plan.tall
    has_below, has_above = g > 0, g < count_g - 1
    y_up, y_down = lax.rem(y + 1, count_y), lax.rem(y + count_y - 1, count_y)
    z_other = lax.rem(z + 1, count_z)

    barrier = pltpu.get_barrier_semaphore()

    def greet(target):
        pl.semaphore_signal(barrier, inc=1, device_id=target, device_id_type=MESH)

    @pl.when(has_below)
    def _():
        greet((g - 1, y, z))

    @pl.when(has_above)
    def _():
        greet((g + 1, y, z))

    greet((g, y_up, z))
    greet((g, y_down, z))
    greet((g, y, z_other))
    pl.semaphore_wait(barrier, 3 + has_below.astype(jnp.int32) + has_above.astype(jnp.int32))

    split = (0, plan.upper // 3 // 8 * 8, plan.upper)
    pieces = [(piece, i) for i in range(3) for piece in range(2)]

    def g_copy(piece, i):
        begin, end = split[piece], min(split[piece + 1], plan.above)
        at = pl.ds(begin * rows, (end - begin) * rows)
        src, dst = (lab.at[at], lab_up.at[at]) if i == 0 else (pot.at[i - 1, at], pot_up.at[i - 1, at])
        sem = 3 * piece + i
        return pltpu.make_async_remote_copy(
            src_ref=src, dst_ref=dst, send_sem=g_send.at[sem], recv_sem=g_recv.at[sem],
            device_id=(g - 1, y, z), device_id_type=MESH)

    @pl.when(has_below)
    def _():
        for piece, i in pieces:
            g_copy(piece, i).start()

    def y_copies(part, i, low, size):
        copies = []
        for up in range(2):
            src, dst, target = (rows, 0, y_up) if up else (STEPS, STEPS + rows, y_down)
            sem = 2 * (3 * part + i) + up
            copy = pltpu.make_async_remote_copy(
                src_ref=main.at[i, pl.ds(src, STEPS), pl.ds(low, size)],
                dst_ref=main.at[i, pl.ds(dst, STEPS), pl.ds(low, size)],
                send_sem=y_send.at[sem], recv_sem=y_recv.at[sem],
                device_id=(g, target, z), device_id_type=MESH)
            copy.start()
            copies.append(copy)
        return copies

    def row_of(ref, i, row, begin, size):
        at = pl.ds(begin * rows + row, size, stride=rows)
        return ref[at].astype(jnp.float32) if i == 0 else ref[i - 1, at]

    y_sent = {}
    for i in range(3):
        for row in range(rows):
            main[i, STEPS + row, 0:own] = row_of(lab if i == 0 else pot, i, row, plan.skip, own)
        y_sent[0, i] = y_copies(0, i, 0, own)

    def z_copy(part, i, low, size):
        for copy in y_sent[part, i]:
            copy.wait_recv()
        lane = lax.broadcasted_iota(jnp.int32, (size, 128), 1)
        for parity in range(2):
            packed = jnp.zeros((size, 128), jnp.float32)
            for slot in range(plan.slots):
                turned = pltpu.roll(main[i, 2 * slot + parity, low : low + size], WIDE * slot + HALF, 1)
                packed = jnp.where((lane >= WIDE * slot) & (lane < WIDE * slot + WIDE), turned, packed)
            pack[i, parity, low : low + size] = packed
        sem = 3 * part + i
        at = (i, slice(None), pl.ds(low, size))
        copy = pltpu.make_async_remote_copy(
            src_ref=pack.at[at], dst_ref=strip.at[at], send_sem=z_send.at[sem], recv_sem=z_recv.at[sem],
            device_id=(g, y, z_other), device_id_type=MESH)
        copy.start()
        return copy

    def enter(piece, i):
        begin, end = split[piece], split[piece + 1]
        filled = min(end, plan.above)

        @pl.when(has_above)
        def _():
            g_copy(piece, i).wait_recv()
            for row in range(rows):
                main[i, STEPS + row, own + begin : own + filled] = row_of(lab_up if i == 0 else pot_up, i, row, begin, filled - begin)
                if end > filled:
                    main[i, STEPS + row, own + filled : own + end] = jnp.zeros((end - filled, 128), jnp.float32)

        @pl.when(jnp.logical_not(has_above))
        def _():
            melt_end = min(end, plan.shift)
            for row in range(rows):
                if i == 0:
                    value = jnp.full((melt_end - begin, 128), 3.0, jnp.float32)
                else:
                    code = codes[pl.ds(begin * rows + row, melt_end - begin, stride=rows)]
                    value = jnp.zeros((melt_end - begin, 128), jnp.float32)
                    for level in range(levels):
                        value = jnp.where(code == level, table[i - 1, level], value)
                main[i, STEPS + row, own + begin : own + melt_end] = value
                if end > melt_end:
                    main[i, STEPS + row, own + melt_end : own + end] = jnp.zeros((end - melt_end, 128), jnp.float32)

        y_sent[1 + piece, i] = y_copies(1 + piece, i, own + begin, end - begin)

    z_sent = []
    for i in range(3):
        enter(0, i)
        enter(1, i)
        z_sent.append(z_copy(0, i, 0, own))
    for piece, i in pieces:
        z_sent.append(z_copy(1 + piece, i, own + split[piece], split[piece + 1] - split[piece]))

    for copy in z_sent:
        copy.wait()
    for copies in y_sent.values():
        for copy in copies:
            copy.wait_send()

    @pl.when(has_below)
    def _():
        for piece, i in pieces:
            g_copy(piece, i).wait_send()


def cell_step(center, sums):
    p, (m0, m1) = center[:4], center[4:]
    around = sums[:3] + [6.0 - (sums[0] + sums[1] + sums[2])]
    third = 0.3 * (m0 + m1) + 0.15
    minus_w = (third + 2.1 * m0, third + 2.1 * m1, third, 3.5 * third - 0.525)
    squares = [v * v for v in p]
    shared = 0.28 - 0.6 * ((squares[0] + squares[1]) + (squares[2] + squares[3]))
    local = [p[a] * ((shared + minus_w[a]) + p[a] * (0.6 * p[a] - minus_w[a])) for a in range(4)]
    mean = 0.25 * ((local[0] + local[1]) + (local[2] + local[3])) - 0.07
    held = [jnp.clip((0.12 * around[a] - mean) + local[a], 0.0, 1.0) for a in range(4)]
    inverse = 1.0 / ((held[0] + held[1]) + (held[2] + held[3]))
    new = [v * inverse for v in held]
    change = [new[a] * new[a] * (1.5 - new[a]) - squares[a] * (1.5 - p[a]) for a in range(4)]
    release = 0.2 * (change[0] + change[1] + change[2]) + 0.7 * change[3]
    mobility = 0.0075 + 0.1425 * p[3]
    new0 = (m0 + mobility * (sums[3] - 6.0 * m0)) - (release + 1.4 * change[0])
    new1 = (m1 + mobility * (sums[4] - 6.0 * m1)) - (release + 1.4 * change[1])
    return new + [new0, new1]


def steps_kernel(plan, count_g, main0, strip0, edge0, phases, potentials, main_a, main_b, strip_a, strip_b, edges):
    g = lax.axis_index("grow")
    is_first, is_last = g == 0, g == count_g - 1
    rows, tall, deep = plan.rows, plan.tall, plan.deep

    def unpack(source, target, index):
        label = source[(0,) + index]
        for a in range(4):
            target[(a,) + index] = jnp.where(label == float(a), 1.0, 0.0)
        for i in range(2):
            target[(4 + i,) + index] = source[(1 + i,) + index]

    def unpack_row(row, carry):
        unpack(main0, main_a, (row,))
        return carry

    lax.fori_loop(0, tall, unpack_row, 0)
    for parity in range(2):
        unpack(strip0, strip_a, (parity,))
        unpack(edge0, edges, (parity,))

    lane = lax.broadcasted_iota(jnp.int32, (8, 128), 1)
    place = lax.broadcasted_iota(jnp.int32, (8, 128), 0)
    at_left, at_right = lane == 0, lane == 127
    inner_left, inner_right = lane % WIDE == HALF - 1, lane % WIDE == HALF

    def grow_sides(ref, index, low, center, top, bottom):
        above = ref[index + (pl.ds(low + 1, 8), slice(None))]
        below = ref[index + (pl.ds(low - 1, 8), slice(None))]
        if top is not None and low <= top < low + 8:
            above = jnp.where((place == top - low) & is_last, center, above)
        if bottom is not None and low <= bottom < low + 8:
            below = jnp.where((place == bottom - low) & is_first, center, below)
        return above + below

    moving = (0, 1, 2, 4, 5)

    def main_tile(src, strips, row, parity, slot, low, top, bottom):
        turn = 128 - (WIDE * slot + HALF)
        center = [src[f, row, pl.ds(low, 8), :] for f in range(6)]
        sums = []
        for f in moving:
            v = center[f]
            near = pltpu.roll(strips[f, parity, pl.ds(low, 8), :], turn, 1)
            right = pltpu.roll(jnp.where(at_left, near, v), 127, 1)
            left = pltpu.roll(jnp.where(at_right, near, v), 1, 1)
            total = grow_sides(src, (f, row), low, v, top, bottom)
            total = total + (src[f, row + 1, pl.ds(low, 8), :] + src[f, row - 1, pl.ds(low, 8), :])
            sums.append(total + (right + left))
        return cell_step(center, sums)

    def strip_tile(strips, parity, low, top, bottom):
        center = [strips[f, parity, pl.ds(low, 8), :] for f in range(6)]
        sums = []
        for f in moving:
            v = center[f]
            edge = edges[f, parity, pl.ds(low, 8), :]
            right = pltpu.roll(jnp.where(inner_right, edge, v), 127, 1)
            left = pltpu.roll(jnp.where(inner_left, edge, v), 1, 1)
            other = strips[f, 1 - parity, pl.ds(low, 8), :]
            across = pltpu.roll(other, WIDE if parity == 0 else 128 - WIDE, 1)
            total = grow_sides(strips, (f, parity), low, v, top, bottom)
            sums.append(total + (other + across) + (right + left))
        return cell_step(center, sums)

    state = (main_a, strip_a, main_b, strip_b)
    for step in range(1, STEPS + 1):
        src, strips, dst, strips_dst = state
        early = step <= STEPS_BEFORE
        top = plan.own - 1 if early else plan.first + plan.planes - 1
        bottom = None if early else plan.first
        if step < STEPS:
            for tile in range(plan.tiles):
                for parity in range(2):
                    low = plan.start + 8 * tile
                    new = strip_tile(strips, parity, low, top, bottom)
                    for f in range(6):
                        strips_dst[f, parity, pl.ds(low, 8), :] = new[f]

            def pair_step(pair, carry):
                for part in range(2):
                    row, parity = 2 * pair + step + part, (step + part) % 2
                    slot = pair + (step + part) // 2
                    turn = WIDE * slot + HALF
                    inside = (lane == turn) | (lane == turn - 1)
                    for tile in range(plan.tiles):
                        low = plan.start + 8 * tile
                        new = main_tile(src, strips, row, parity, slot, low, top, bottom)
                        for f in range(6):
                            dst[f, row, pl.ds(low, 8), :] = new[f]
                            if f in moving and step < STEPS - 1:
                                at = (f, parity, pl.ds(low, 8), slice(None))
                                edges[at] = jnp.where(inside, pltpu.roll(new[f], turn, 1), edges[at])
                return carry

            lax.fori_loop(0, (tall - 2 * step) // 2, pair_step, 0)
        else:
            def pair_last(pair, carry):
                for part in range(2):
                    row, parity = 2 * pair + part, (STEPS + part) % 2
                    slot = pair + (STEPS + part) // 2
                    for tile in range(plan.planes // 8):
                        low = plan.first + 8 * tile
                        new = main_tile(src, strips, row + STEPS, parity, slot, low, top, bottom)
                        at = pl.ds(8 * tile * rows + row, 8, stride=rows)
                        for f in range(4):
                            phases[f, at, :] = new[f]
                        for i in range(2):
                            potentials[i, at, :] = new[4 + i]
                return carry

            lax.fori_loop(0, rows // 2, pair_last, 0)
        if step == STEPS_BEFORE:
            melt = (slice(plan.own, plan.own + plan.shift), slice(None))

            @pl.when(is_last)
            def _():
                def fill(row, carry):
                    unpack(main0, dst, (row,) + melt)
                    return carry

                lax.fori_loop(0, tall, fill, 0)
                for parity in range(2):
                    unpack(strip0, strips_dst, (parity,) + melt)
                    unpack(edge0, edges, (parity,) + melt)

        state = (dst, strips_dst, src, strips)


def on_device(mesh_shape, labels, potential, melt_codes, melt_table):
    planes, rows, width = labels.shape
    shift, levels = melt_codes.shape[0], melt_table.shape[1]
    plan = Plan(planes, rows, shift)
    flat = planes * rows
    vmem = pl.BlockSpec(memory_space=pltpu.VMEM)
    smem = pl.BlockSpec(memory_space=pltpu.SMEM)
    f32 = jnp.float32
    dma = pltpu.SemaphoreType.DMA
    main0, strip0, edge0 = pl.pallas_call(
        functools.partial(gather_kernel, plan, mesh_shape, levels),
        out_shape=(
            pltpu.VMEM((3, plan.tall, plan.deep, width), f32),
            pltpu.VMEM((3, 2, plan.deep, width), f32),
            pltpu.VMEM((3, 2, plan.deep, width), f32),
        ),
        in_specs=[vmem, vmem, vmem, smem],
        out_specs=(vmem, vmem, vmem),
        scratch_shapes=[
            pltpu.VMEM((plan.above * rows, width), jnp.int32),
            pltpu.VMEM((2, plan.above * rows, width), f32),
            dma((6,)), dma((6,)), dma((18,)), dma((18,)), dma((9,)), dma((9,)),
        ],
        compiler_params=pltpu.CompilerParams(collective_id=0, has_side_effects=True),
        name="gather",
    )(labels.reshape(flat, width), potential.reshape(2, flat, width), melt_codes.reshape(shift * rows, width), melt_table)
    main0, strip0, edge0 = (pltpu.with_memory_space_constraint(v, pltpu.VMEM) for v in (main0, strip0, edge0))
    phases, potentials = pl.pallas_call(
        functools.partial(steps_kernel, plan, mesh_shape[0]),
        out_shape=(
            jax.ShapeDtypeStruct((4, flat, width), f32),
            jax.ShapeDtypeStruct((2, flat, width), f32),
        ),
        in_specs=[vmem, vmem, vmem],
        out_specs=(vmem, vmem),
        scratch_shapes=[
            pltpu.VMEM((6, plan.tall, plan.deep, width), f32),
            pltpu.VMEM((6, plan.tall, plan.deep, width), f32),
            pltpu.VMEM((6, 2, plan.deep, width), f32),
            pltpu.VMEM((6, 2, plan.deep, width), f32),
            pltpu.VMEM((6, 2, plan.deep, width), f32),
        ],
        name="steps",
    )(main0, strip0, edge0)
    return phases.reshape(4, planes, rows, width), potentials.reshape(2, planes, rows, width)


def solution(mesh):
    mesh_shape = tuple(mesh.shape[axis] for axis in ("grow", "gy", "gz"))
    return jax.shard_map(
        functools.partial(on_device, mesh_shape),
        mesh=mesh,
        in_specs=(P("grow", "gy", "gz"), P(None, "grow", "gy", "gz"), P(None, "gy", "gz"), P()),
        out_specs=(P(None, "grow", "gy", "gz"), P(None, "grow", "gy", "gz")),
        check_vma=False,
    )
```

profile of v0, /device:TPU:0, one launch (start us, length us, event | category | flops | bytes accessed | tf_op | source)
XLA Modules:
  0.0 31.3 jit_solution(4246636901415235947)
XLA Ops:
  0.6 17.4 %gather.1 = (f32[3,18,48,128]{3,2,1,0:T(8,128)S(1)}, f32[3,2,48,128]{3,2,1,0:T(8,128)S(1)}, f32[3,2,48,128]{3,2,1,0:T(8,128)S(1)}) custom-call(s32[256,128]{1,0:T(8,128)} %bitcast.6, f32[2,256,128]{2,1,0:T(8,128)} %bitcast.5, s32[128,128]{1,0:T(8,128)} %bitcast.7, f32[2,8]{1,0:T(2,128)} %table.1), custom_call_target="tpu_custom_call" | custom-call | tf_op jit(solution)/shard_map/gather/pallas_call | solution.py:325
  18.1 13.2 %steps.1 = (f32[4,256,128]{2,1,0:T(8,128)}, f32[2,256,128]{2,1,0:T(8,128)}) custom-call(f32[3,18,48,128]{3,2,1,0:T(8,128)S(1)} %get-tuple-element.7.main0, f32[3,2,48,128]{3,2,1,0:T(8,128)S(1)} %get-tuple-element.8.strip0, f32[3,2,48,128]{3,2,1,0:T(8,128)S(1)} %get-tuple-element.9.edge0), custom_call_target="tpu_custom_call" | custom-call | tf_op jit(solution)/shard_map/steps/pallas_call | solution.py:343
where the time goes:
time: 31.8 us; the launch traced here: 31.3 us
  Pallas kernels  30.6 us (96%)
  between operations  0.64 us (2%)
    pallas_call x1, Pallas kernels, on_device(): pl.pallas_call(functools.partial(gather_kernel, plan, mesh_shape, levels)...  17.4 us
    pallas_call x1, Pallas kernels, on_device(): pl.pallas_call(functools.partial(steps_kernel, plan, mesh_shape[0]), out_...  13.2 us

commit v1 on v0

v1 whole, which is shorter than its diff:
```python
import functools

import jax
import jax.numpy as jnp
from jax import lax
from jax.experimental import pallas as pl
from jax.experimental.pallas import tpu as pltpu
from jax.sharding import PartitionSpec as P

STEPS_BEFORE = 3
STEPS_AFTER = 2
STEPS = STEPS_BEFORE + STEPS_AFTER
HALF = 9
SLOT = 2 * HALF
GROUPS = 3
FIELDS = 11
MOVING = 5
PAD = 8
MESH = pl.DeviceIdType.MESH

LAM = 0.12
BETA = 5.0 / LAM**2
MU = 17.5 / (LAM * BETA)
OWN = (1.0 / LAM - 6.0) / BETA
TILT = 1.25 / (LAM * BETA)
BACK = 0.2 * MU / LAM**3


class Plan:
    def __init__(self, planes, rows, shift):
        self.planes, self.rows, self.shift = planes, rows, shift
        self.low = shift - STEPS + 1
        self.chunks = planes // 8 + 1
        self.deep = 8 * (self.chunks + 2)
        self.above = shift + STEPS
        self.tall = rows + 2 * STEPS

    def at(self, plane):
        return plane - self.low + PAD


def phase_state(label, pot):
    q = [jnp.where(label == float(a), LAM, 0.0) for a in range(3)]
    y = [jnp.where(label == float(a), LAM * BETA * OWN, 0.0) for a in range(3)]
    liquid = label == 3.0
    mob = jnp.where(liquid, 0.15, 0.0075)
    u = [MU * v for v in pot]
    comp = [jnp.where(liquid, 0.35 * MU, jnp.where(label == float(i), 0.8 * MU, 0.1 * MU)) for i in range(2)]
    rest = [(u[i] + comp[i]) - (6.0 * mob) * u[i] for i in range(2)]
    return q + u + y + rest + [mob]


def clip_step(sums, y):
    x = [sums[a] + y[a] for a in range(3)]
    x.append(1.0 - (x[0] + x[1] + x[2]))
    held = [jnp.clip(v, 0.0, 1.0) for v in x]
    return held, 1.0 / ((held[0] + held[1]) + (held[2] + held[3]))


def cell_step(sums, y, rest, mob):
    held, inverse = clip_step(sums, y)
    total = [rest[i] + mob * sums[3 + i] for i in range(2)]
    scaled = LAM * inverse
    q = [v * scaled for v in held]
    square = [v * v for v in q]
    h = [square[a] * (1.5 * LAM - q[a]) for a in range(4)]
    shared = BACK * ((h[0] + h[1]) + (h[2] + 3.5 * h[3]))
    u = [(total[i] - shared) - (7.0 * BACK) * h[i] for i in range(2)]
    both = u[0] + u[1]
    third = both * (1.0 / 7.0) + TILT
    pull = [third + u[0], third + u[1], third, 0.5 * both]
    well = OWN - ((square[0] + square[1]) + (square[2] + square[3]))
    local = [q[a] * ((well + square[a]) + pull[a] * (LAM - q[a])) for a in range(4)]
    mean = 0.25 * ((local[0] + local[1]) + (local[2] + local[3])) - 0.07 / BETA
    y = [BETA * (local[a] - mean) for a in range(3)]
    mob = 0.0075 + (0.1425 / LAM) * q[3]
    six = 6.0 * mob
    rest = [total[i] - six * u[i] for i in range(2)]
    return q[:3] + u + y + rest + [mob]


def last_step(sums, y, rest, mob):
    held, inverse = clip_step(sums, y)
    p = [v * inverse for v in held]
    h = [v * v * (1.5 - v) for v in p]
    shared = 0.2 * ((h[0] + h[1]) + (h[2] + 3.5 * h[3]))
    total = [(rest[i] + mob * sums[3 + i]) * (1.0 / MU) for i in range(2)]
    return p, [(total[i] - shared) - 1.4 * h[i] for i in range(2)]


def lanes():
    return lax.broadcasted_iota(jnp.int32, (8, 128), 1)


def load(ref, *index):
    return ref[index]


def main_sums(state, near, row, low, at_left, at_right):
    slot, group = (row // GROUPS, row % GROUPS) if isinstance(row, int) else (lax.div(row, GROUPS), lax.rem(row, GROUPS))
    turn = 128 - (SLOT * slot + HALF // 2 + 1)
    sums = []
    for f in range(MOVING):
        v = state[f, row, pl.ds(low, 8), :]
        edge = pltpu.roll(near[f, group, pl.ds(low, 8), :], turn, 1)
        right = pltpu.roll(jnp.where(at_left, edge, v), 127, 1)
        left = pltpu.roll(jnp.where(at_right, edge, v), 1, 1)
        grow = state[f, row, pl.ds(low + 1, 8), :] + state[f, row, pl.ds(low - 1, 8), :]
        side = state[f, row + 1, pl.ds(low, 8), :] + state[f, row - 1, pl.ds(low, 8), :]
        sums.append((grow + side) + (right + left))
    return sums


def center(state, row, low):
    y = [state[MOVING + a, row, pl.ds(low, 8), :] for a in range(3)]
    rest = [state[MOVING + 3 + i, row, pl.ds(low, 8), :] for i in range(2)]
    return y, rest, state[FIELDS - 1, row, pl.ds(low, 8), :]


def near_of(v, swap):
    return jnp.where(swap, pltpu.roll(v, 128 - (HALF - 1), 1), v)


def front_kernel(
    plan, mesh_shape, levels, lab, pot, codes, table, last_state, last_near,
    lab_up, pot_up, raw, pack, strip, states, strips, nears,
    g_send, g_recv, y_send, y_recv, z_send, z_recv,
):
    g, y, z = lax.axis_index("grow"), lax.axis_index("gy"), lax.axis_index("gz")
    count_g, count_y, count_z = mesh_shape
    rows, tall, planes, shift = plan.rows, plan.tall, plan.planes, plan.shift
    has_below, has_above = g > 0, g < count_g - 1
    is_first, is_last = g == 0, g == count_g - 1
    y_up, y_down = lax.rem(y + 1, count_y), lax.rem(y + count_y - 1, count_y)
    z_other = lax.rem(z + 1, count_z)
    chunks = plan.chunks

    barrier = pltpu.get_barrier_semaphore()

    def greet(target):
        pl.semaphore_signal(barrier, inc=1, device_id=target, device_id_type=MESH)

    @pl.when(has_below)
    def _():
        greet((g - 1, y, z))

    @pl.when(has_above)
    def _():
        greet((g + 1, y, z))

    greet((g, y_up, z))
    greet((g, y_down, z))
    greet((g, y, z_other))
    pl.semaphore_wait(barrier, 3 + has_below.astype(jnp.int32) + has_above.astype(jnp.int32))

    first_up = (planes - plan.low) // 8
    cut = 8 * (first_up + 1) - (planes - plan.low)
    splits = [0] + list(range(cut, plan.above - 1, 8)) + [plan.above]
    pieces = len(splits) - 1

    def g_copies(piece):
        begin, end = splits[piece], splits[piece + 1]
        at = pl.ds(begin * rows, (end - begin) * rows)
        copies = []
        for i in range(3):
            src, dst = (lab.at[at], lab_up.at[at]) if i == 0 else (pot.at[i - 1, at], pot_up.at[i - 1, at])
            sem = 3 * piece + i
            copies.append(pltpu.make_async_remote_copy(
                src_ref=src, dst_ref=dst, send_sem=g_send.at[sem], recv_sem=g_recv.at[sem],
                device_id=(g - 1, y, z), device_id_type=MESH))
        return copies

    @pl.when(has_below)
    def _():
        for piece in range(pieces):
            for copy in g_copies(piece):
                copy.start()

    def y_copies(chunk):
        copies = []
        for up in range(2):
            src, dst, target = (rows, 0, y_up) if up else (STEPS, STEPS + rows, y_down)
            sem = 2 * chunk + up
            at = pl.ds(PAD + 8 * chunk, 8)
            copies.append(pltpu.make_async_remote_copy(
                src_ref=raw.at[:, pl.ds(src, STEPS), at], dst_ref=raw.at[:, pl.ds(dst, STEPS), at],
                send_sem=y_send.at[sem], recv_sem=y_recv.at[sem],
                device_id=(g, target, z), device_id_type=MESH))
        return copies

    def z_copy(chunk):
        at = pl.ds(PAD + 8 * chunk, 8)
        return pltpu.make_async_remote_copy(
            src_ref=pack.at[:, :, at], dst_ref=strip.at[:, :, at],
            send_sem=z_send.at[chunk], recv_sem=z_recv.at[chunk],
            device_id=(g, y, z_other), device_id_type=MESH)

    def row_of(labels, pots, i, row, begin, size):
        at = pl.ds(begin * rows + row, size, stride=rows)
        return labels[at].astype(jnp.float32) if i == 0 else pots[i - 1, at]

    def fill(labels, pots, begin, size, to):
        for i in range(3):
            for row in range(rows):
                raw[i, STEPS + row, to : to + size] = row_of(labels, pots, i, row, begin, size)

    def fill_melt(begin, size, to, copies=1):
        for row in range(rows):
            at = pl.ds(to, size * copies)
            code = codes[pl.ds(begin * rows + row, size, stride=rows)]
            raw[0, STEPS + row, at] = jnp.full((size * copies, 128), 3.0, jnp.float32)
            for i in range(2):
                value = jnp.zeros((size, 128), jnp.float32)
                for level in range(levels):
                    value = jnp.where(code == level, table[i, level], value)
                raw[1 + i, STEPS + row, at] = jnp.broadcast_to(value, (size * copies, 128))

    def enter(piece):
        begin, end = splits[piece], splits[piece + 1]
        to = plan.at(planes + begin)

        @pl.when(has_above)
        def _():
            for copy in g_copies(piece):
                copy.wait_recv()
            size = min(end - begin, 8)
            fill(lab_up, pot_up, begin, size, to)
            if end - begin > 8:
                fill(lab_up, pot_up, end - 1, 1, to + 8)

        @pl.when(is_last)
        def _():
            if piece == 0:
                fill(lab, pot, planes - 1, 1, to)
                fill_melt(0, end - 1, to + 1)
            else:
                size = min(end - 1, shift) - (begin - 1)
                fill_melt(begin - 1, size, to)
                if end - begin > size:
                    fill_melt(shift - 1, 1, to + size, end - begin - size)

    def pack_chunk(chunk):
        at = pl.ds(PAD + 8 * chunk, 8)
        lane = lanes()
        for i in range(3):
            for group in range(GROUPS):
                packed = jnp.zeros((8, 128), jnp.float32)
                for slot in range(tall // GROUPS):
                    v = raw[i, GROUPS * slot + group, at]
                    first = SLOT * slot
                    packed = jnp.where(lane >= first, pltpu.roll(v, first + HALF // 2 + 1, 1), packed)
                    packed = jnp.where(lane >= first + HALF, pltpu.roll(v, first + HALF + HALF // 2, 1), packed)
                pack[i, group, at] = packed

    def send_z(chunk):
        for copy in y_copies(chunk):
            copy.wait_recv()
        pack_chunk(chunk)
        z_copy(chunk).start()

    def send_y(chunk):
        for copy in y_copies(chunk):
            copy.start()

    place = lanes() % SLOT
    from_other = (place < HALF // 2 + 1) | (place >= SLOT - HALF // 2 - 1)
    swap = place == HALF // 2 + 1

    def unpack_rows(to, begin, end):
        def body(row, carry):
            at = pl.ds(to, 8)
            new = phase_state(raw[0, row, at], [raw[1, row, at], raw[2, row, at]])
            for f in range(FIELDS):
                states[0, f, row, at] = new[f]
            return carry

        lax.fori_loop(begin, end, body, 0)

    def unpack_strips(source_low, target_low, state, near):
        for group in range(GROUPS):
            at = pl.ds(source_low, 8)
            value = [jnp.where(from_other, strip[i, group, at], pack[i, group, at]) for i in range(3)]
            new = phase_state(value[0], value[1:])
            to = pl.ds(target_low, 8)
            for f in range(FIELDS):
                state[f, group, to] = new[f]
            for f in range(MOVING):
                near[f, group, to] = near_of(new[f], swap)

    def unpack(chunk):
        z_copy(chunk).wait_recv()
        to = PAD + 8 * chunk
        unpack_rows(to, 0, tall)
        unpack_strips(to, to, strips.at[0], nears.at[0])

    at_left, at_right = lanes() == 0, lanes() == 127

    def near_ref(step):
        return nears.at[step] if step < STEPS - 1 else last_near

    def state_ref(step):
        return states.at[step] if step < STEPS - 1 else last_state

    def strip_step(step, low):
        src = strips.at[step - 1]
        at = pl.ds(low, 8)
        for group in range(GROUPS):
            sums = []
            for f in range(MOVING):
                v = src[f, group, at]
                up = src[f, (group + 1) % GROUPS, at]
                down = src[f, (group + 2) % GROUPS, at]
                if group == 0:
                    down = pltpu.roll(down, SLOT, 1)
                if group == GROUPS - 1:
                    up = pltpu.roll(up, 128 - SLOT, 1)
                total = src[f, group, pl.ds(low + 1, 8)] + src[f, group, pl.ds(low - 1, 8)]
                sums.append((total + (up + down)) + (pltpu.roll(v, 127, 1) + pltpu.roll(v, 1, 1)))
            new = cell_step(sums, *center(src, group, low))
            if step < STEPS - 1:
                for f in range(FIELDS):
                    strips[step, f, group, at] = new[f]
            for f in range(MOVING):
                near_ref(step)[f, group, at] = near_of(new[f], swap)

    def row_step(step, row, low):
        src, near = states.at[step - 1], nears.at[step - 1]
        sums = main_sums(src, near, row, low, at_left, at_right)
        new = cell_step(sums, *center(src, row, low))
        for f in range(FIELDS):
            state_ref(step)[f, row, pl.ds(low, 8), :] = new[f]

    def copy_plane(step, begin, end):
        def body(row, carry):
            for f in range(MOVING):
                state_ref(step)[f, row, pl.ds(end, 1)] = state_ref(step)[f, row, pl.ds(begin, 1)]
            return carry

        lax.fori_loop(step, tall - step, body, 0)
        if step < STEPS - 1:
            for group in range(GROUPS):
                for f in range(MOVING):
                    strips[step, f, group, pl.ds(end, 1)] = strips[step, f, group, pl.ds(begin, 1)]
        for group in range(GROUPS):
            for f in range(MOVING):
                near_ref(step)[f, group, pl.ds(end, 1)] = near_ref(step)[f, group, pl.ds(begin, 1)]

    def melt_fill(low):
        step = STEPS_BEFORE

        def body(row, carry):
            at = pl.ds(low + 1, 8)
            new = phase_state(raw[0, row, at], [raw[1, row, at], raw[2, row, at]])
            for f in range(FIELDS):
                states[step, f, row, pl.ds(low, 8)] = new[f]
            return carry

        lax.fori_loop(step, tall - step, body, 0)
        unpack_strips(low + 1, low, strips.at[step], nears.at[step])

    def advance(step, low):
        strip_step(step, low)
        count = (tall - 2 * step) // 2

        def body(half, carry):
            for part in range(count):
                row_step(step, step + count * half + part, low)
            return carry

        lax.fori_loop(0, 2, body, 0)

    first_plane, top_plane = plan.at(shift), plan.at(planes)

    def prologue():
        fill(lab, pot, plan.low - PAD, 8, 0)
        for chunk in range(first_up):
            fill(lab, pot, plan.low + 8 * chunk, 8, PAD + 8 * chunk)
            send_y(chunk)
        done = plan.low + 8 * first_up
        fill(lab, pot, done, planes - done, PAD + 8 * first_up)
        unpack_rows(0, STEPS, STEPS + rows)

    prologue()

    def before(stage):
        if stage == 0:
            for chunk in range(first_up):
                send_z(chunk)
            for piece in range(pieces):
                enter(piece)
                send_y(first_up + piece)
            send_z(first_up)
            unpack(0)
        unpack(stage + 1)

    def middle(stage):
        chunk = first_up + 1 + stage
        if chunk < chunks:
            send_z(chunk)

    def stage_body(stage, carry):
        def run_at(action):
            for at in range(chunks):
                @pl.when(stage == at)
                def _():
                    action(at)

        def before_or_end(at):
            if at < chunks - 1:
                before(at)
            else:
                unpack_rows(PAD + 8 * chunks, STEPS, STEPS + rows)

        run_at(before_or_end)
        for step in range(1, STEPS):
            low = PAD + 1 + 8 * stage - step
            if step <= STEPS_BEFORE:
                top = (top_plane - (PAD + 1 - step)) // 8
                pl.when((stage <= top) | jnp.logical_not(is_last))(functools.partial(advance, step, low))
            else:
                advance(step, low)

            def planes_at(plane):
                return (plane - (PAD + 1 - step)) // 8

            if step < STEPS_BEFORE:
                @pl.when(is_last & (stage == planes_at(top_plane)))
                def _():
                    copy_plane(step, top_plane - 1, top_plane)
            if step == STEPS_BEFORE:
                @pl.when(is_first & (stage == planes_at(first_plane)))
                def _():
                    copy_plane(step, first_plane, first_plane - 1)

                @pl.when(is_last & (stage == planes_at(top_plane)))
                def _():
                    melt_fill(top_plane)

                @pl.when(is_last & (stage > planes_at(top_plane)))
                def _():
                    melt_fill(jnp.minimum(low, top_plane + shift + 1 - 8))
            if step == STEPS - 1:
                @pl.when(is_first & (stage == planes_at(first_plane)))
                def _():
                    copy_plane(step, first_plane, first_plane - 1)

                @pl.when(is_last & (stage == planes_at(first_plane + planes)))
                def _():
                    copy_plane(step, first_plane + planes - 1, first_plane + planes)
            if step == 2:
                run_at(middle)
        return carry

    lax.fori_loop(0, chunks, stage_body, 0)

    for chunk in range(chunks):
        for copy in y_copies(chunk):
            copy.wait_send()
        z_copy(chunk).wait_send()

    @pl.when(has_below)
    def _():
        for piece in range(pieces):
            for copy in g_copies(piece):
                copy.wait_send()


def last_kernel(plan, state, near, phases, potentials, p_out, m_out, sems):
    rows, planes = plan.rows, plan.planes
    at_left, at_right = lanes() == 0, lanes() == 127
    copies = []
    for tile in range(planes // 8):
        low = plan.at(plan.shift) + 8 * tile
        for row in range(rows):
            sums = main_sums(state, near, STEPS + row, low, at_left, at_right)
            p, m = last_step(sums, *center(state, STEPS + row, low))
            at = pl.ds(8 * tile * rows + row, 8, stride=rows)
            for f in range(4):
                p_out[f, at, :] = p[f]
            for i in range(2):
                m_out[i, at, :] = m[i]
        at = pl.ds(8 * tile * rows, 8 * rows)
        for i, (src, dst) in enumerate(((p_out, phases), (m_out, potentials))):
            copy = pltpu.make_async_copy(src.at[:, at], dst.at[:, at], sems.at[2 * tile + i])
            copy.start()
            copies.append(copy)
    for copy in copies:
        copy.wait()


def on_device(mesh_shape, labels, potential, melt_codes, melt_table):
    planes, rows, width = labels.shape
    shift, levels = melt_codes.shape[0], melt_table.shape[1]
    plan = Plan(planes, rows, shift)
    flat = planes * rows
    vmem = pl.BlockSpec(memory_space=pltpu.VMEM)
    smem = pl.BlockSpec(memory_space=pltpu.SMEM)
    hbm = pl.BlockSpec(memory_space=pl.ANY)
    f32 = jnp.float32
    dma = pltpu.SemaphoreType.DMA
    deep, tall, chunks = plan.deep, plan.tall, plan.chunks
    state, near = pl.pallas_call(
        functools.partial(front_kernel, plan, mesh_shape, levels),
        out_shape=(
            pltpu.VMEM((FIELDS, tall, deep, width), f32),
            pltpu.VMEM((MOVING, GROUPS, deep, width), f32),
        ),
        in_specs=[vmem, vmem, vmem, smem],
        out_specs=(vmem, vmem),
        scratch_shapes=[
            pltpu.VMEM((plan.above * rows, width), jnp.int32),
            pltpu.VMEM((2, plan.above * rows, width), f32),
            pltpu.VMEM((3, tall, deep, width), f32),
            pltpu.VMEM((3, GROUPS, deep, width), f32),
            pltpu.VMEM((3, GROUPS, deep, width), f32),
            pltpu.VMEM((STEPS - 1, FIELDS, tall, deep, width), f32),
            pltpu.VMEM((STEPS - 1, FIELDS, GROUPS, deep, width), f32),
            pltpu.VMEM((STEPS - 1, MOVING, GROUPS, deep, width), f32),
            dma((3 * chunks,)), dma((3 * chunks,)), dma((2 * chunks,)), dma((2 * chunks,)), dma((chunks,)), dma((chunks,)),
        ],
        compiler_params=pltpu.CompilerParams(collective_id=0, has_side_effects=True, vmem_limit_bytes=48 << 20),
        name="front",
    )(labels.reshape(flat, width), potential.reshape(2, flat, width), melt_codes.reshape(shift * rows, width), melt_table)
    state, near = (pltpu.with_memory_space_constraint(v, pltpu.VMEM) for v in (state, near))
    phases, potentials = pl.pallas_call(
        functools.partial(last_kernel, plan),
        out_shape=(
            jax.ShapeDtypeStruct((4, flat, width), f32),
            jax.ShapeDtypeStruct((2, flat, width), f32),
        ),
        in_specs=[vmem, vmem],
        out_specs=(hbm, hbm),
        scratch_shapes=[
            pltpu.VMEM((4, flat, width), f32),
            pltpu.VMEM((2, flat, width), f32),
            dma((2 * (planes // 8),)),
        ],
        compiler_params=pltpu.CompilerParams(vmem_limit_bytes=8 << 20),
        name="last",
    )(state, near)
    return phases.reshape(4, planes, rows, width), potentials.reshape(2, planes, rows, width)


def solution(mesh):
    mesh_shape = tuple(mesh.shape[axis] for axis in ("grow", "gy", "gz"))
    return jax.shard_map(
        functools.partial(on_device, mesh_shape),
        mesh=mesh,
        in_specs=(P("grow", "gy", "gz"), P(None, "grow", "gy", "gz"), P(None, "gy", "gz"), P()),
        out_specs=(P(None, "grow", "gy", "gz"), P(None, "grow", "gy", "gz")),
        check_vma=False,
    )
```

time: 31.8 us -> 40.9 us (1.29)
  Pallas kernels: 30.6 us -> 38.4 us
  local copies, waits for them, and re-layouts: 0 us -> 1.51 us
    pallas_call x2, Pallas kernels: 30.6 us -> 38.4 us  [the longest x1 29.8 us: on_device(): pl.pallas_call(functools.partial(front_kernel, plan, mesh_shape, levels),...]
    unnamed x0 -> x4, local copies, waits for them, and re-layouts: none -> 1.51 us
where the time goes in v1:
time: 40.9 us; the launch traced here: 40.6 us
  Pallas kernels  38.4 us (94%)
  local copies, waits for them, and re-layouts  1.51 us (4%)
  between operations  0.65 us (2%)
    pallas_call x1, Pallas kernels, on_device(): pl.pallas_call(functools.partial(front_kernel, plan, mesh_shape, levels),...  29.8 us
    pallas_call x1, Pallas kernels, on_device(): pl.pallas_call(functools.partial(last_kernel, plan), out_shape=(jax.Shape...  8.63 us
    unnamed x4, local copies, waits for them, and re-layouts  1.51 us

profile of v1, /device:TPU:0, one launch (start us, length us, event | category | flops | bytes accessed | tf_op | source)
XLA Modules:
  0.0 40.6 jit_solution(17427490752122449082)
XLA Ops:
  0.6 0.0 copy-start
  0.6 0.8 %copy-done = s32[16,8,128]{2,1,0:T(8,128)S(1)} copy-done((s32[16,8,128]{2,1,0:T(8,128)S(1)}, s32[16,8,128]{2,1,0:T(8,128)}, u32[]{:S(2)}) %copy-start) | copy-done | bytes 65560
  1.5 0.0 copy-start.1
  1.5 0.7 %copy-done.1 = f32[2,8]{1,0:T(2,128)S(1)} copy-done((f32[2,8]{1,0:T(2,128)S(1)}, f32[2,8]{1,0:T(2,128)}, u32[]{:S(2)}) %copy-start.1) | copy-done | bytes 88
  2.2 29.8 %front.1 = (f32[11,18,56,128]{3,2,1,0:T(8,128)S(1)}, f32[5,3,56,128]{3,2,1,0:T(8,128)S(1)}) custom-call(s32[256,128]{1,0:T(8,128)} %bitcast.7, f32[2,256,128]{2,1,0:T(8,128)} %bitcast.6, s32[128,128]{1,0:T(8,128)S(1)} %bitcast.5, f32[2,8]{1,0:T(2,128)S(1)} %copy-done.1), custom_call_target="tpu_custom_call" | custom-call | tf_op jit(solution)/shard_map/front/pallas_call | solution.py:502
  31.9 8.6 %last.1 = (f32[4,256,128]{2,1,0:T(8,128)}, f32[2,256,128]{2,1,0:T(8,128)}) custom-call(f32[11,18,56,128]{3,2,1,0:T(8,128)S(1)} %get-tuple-element.6.state, f32[5,3,56,128]{3,2,1,0:T(8,128)S(1)} %get-tuple-element.7.near), custom_call_target="tpu_custom_call" | custom-call | tf_op jit(solution)/shard_map/last/pallas_call | solution.py:525
Async XLA Ops:
  0.6 0.8 %copy-start = (s32[16,8,128]{2,1,0:T(8,128)S(1)}, s32[16,8,128]{2,1,0:T(8,128)}, u32[]{:S(2)}) copy-start(s32[16,8,128]{2,1,0:T(8,128)} %param.6) | copy-start | bytes 196612
  1.5 0.7 %copy-start.1 = (f32[2,8]{1,0:T(2,128)S(1)}, f32[2,8]{1,0:T(2,128)}, u32[]{:S(2)}) copy-start(f32[2,8]{1,0:T(2,128)} %table.1) | copy-start | bytes 196

commit v2 on v1

v2 whole, which is shorter than its diff:
```python
import functools

import jax
import jax.numpy as jnp
from jax import lax
from jax.experimental import pallas as pl
from jax.experimental.pallas import tpu as pltpu
from jax.sharding import PartitionSpec as P

STEPS_BEFORE = 3
STEPS_AFTER = 2
STEPS = STEPS_BEFORE + STEPS_AFTER
HALF = 9
SLOT = 2 * HALF
GROUPS = 3
FIELDS = 11
MOVING = 5
PAD = 8
MESH = pl.DeviceIdType.MESH

LAM = 0.12
BETA = 5.0 / LAM**2
MU = 17.5 / (LAM * BETA)
OWN = (1.0 / LAM - 6.0) / BETA
TILT = 1.25 / (LAM * BETA)
BACK = 0.2 * MU / LAM**3


class Plan:
    def __init__(self, planes, rows, shift):
        self.planes, self.rows, self.shift = planes, rows, shift
        self.low = shift - STEPS + 1
        self.chunks = planes // 8 + 1
        self.deep = 8 * (self.chunks + 2)
        self.above = shift + STEPS
        self.tall = rows + 2 * STEPS

    def at(self, plane):
        return plane - self.low + PAD


def phase_state(label, pot):
    q = [jnp.where(label == float(a), LAM, 0.0) for a in range(3)]
    y = [jnp.where(label == float(a), LAM * BETA * OWN, 0.0) for a in range(3)]
    liquid = label == 3.0
    mob = jnp.where(liquid, 0.15, 0.0075)
    u = [MU * v for v in pot]
    comp = [jnp.where(liquid, 0.35 * MU, jnp.where(label == float(i), 0.8 * MU, 0.1 * MU)) for i in range(2)]
    rest = [(u[i] + comp[i]) - (6.0 * mob) * u[i] for i in range(2)]
    return q + u + y + rest + [mob]


def clip_step(sums, y):
    x = [sums[a] + y[a] for a in range(3)]
    x.append(1.0 - (x[0] + x[1] + x[2]))
    held = [jnp.clip(v, 0.0, 1.0) for v in x]
    return held, 1.0 / ((held[0] + held[1]) + (held[2] + held[3]))


def cell_step(sums, y, rest, mob):
    held, inverse = clip_step(sums, y)
    total = [rest[i] + mob * sums[3 + i] for i in range(2)]
    scaled = LAM * inverse
    q = [v * scaled for v in held]
    square = [v * v for v in q]
    h = [square[a] * (1.5 * LAM - q[a]) for a in range(4)]
    shared = BACK * ((h[0] + h[1]) + (h[2] + 3.5 * h[3]))
    u = [(total[i] - shared) - (7.0 * BACK) * h[i] for i in range(2)]
    both = u[0] + u[1]
    third = both * (1.0 / 7.0) + TILT
    pull = [third + u[0], third + u[1], third, 0.5 * both]
    well = OWN - ((square[0] + square[1]) + (square[2] + square[3]))
    local = [q[a] * ((well + square[a]) + pull[a] * (LAM - q[a])) for a in range(4)]
    mean = 0.25 * ((local[0] + local[1]) + (local[2] + local[3])) - 0.07 / BETA
    y = [BETA * (local[a] - mean) for a in range(3)]
    mob = 0.0075 + (0.1425 / LAM) * q[3]
    six = 6.0 * mob
    rest = [total[i] - six * u[i] for i in range(2)]
    return q[:3] + u + y + rest + [mob]


def last_step(sums, y, rest, mob):
    held, inverse = clip_step(sums, y)
    p = [v * inverse for v in held]
    h = [v * v * (1.5 - v) for v in p]
    shared = 0.2 * ((h[0] + h[1]) + (h[2] + 3.5 * h[3]))
    total = [(rest[i] + mob * sums[3 + i]) * (1.0 / MU) for i in range(2)]
    return p, [(total[i] - shared) - 1.4 * h[i] for i in range(2)]


def lanes():
    return lax.broadcasted_iota(jnp.int32, (8, 128), 1)


def main_sums(state, near, row, low, at_left, at_right):
    slot, group = (row // GROUPS, row % GROUPS) if isinstance(row, int) else (lax.div(row, GROUPS), lax.rem(row, GROUPS))
    turn = 128 - (SLOT * slot + HALF // 2 + 1)
    sums = []
    for f in range(MOVING):
        v = state[f, row, pl.ds(low, 8), :]
        edge = pltpu.roll(near[f, group, pl.ds(low, 8), :], turn, 1)
        right = pltpu.roll(jnp.where(at_left, edge, v), 127, 1)
        left = pltpu.roll(jnp.where(at_right, edge, v), 1, 1)
        grow = state[f, row, pl.ds(low + 1, 8), :] + state[f, row, pl.ds(low - 1, 8), :]
        side = state[f, row + 1, pl.ds(low, 8), :] + state[f, row - 1, pl.ds(low, 8), :]
        sums.append((grow + side) + (right + left))
    return sums


def center(state, row, low):
    y = [state[MOVING + a, row, pl.ds(low, 8), :] for a in range(3)]
    rest = [state[MOVING + 3 + i, row, pl.ds(low, 8), :] for i in range(2)]
    return y, rest, state[FIELDS - 1, row, pl.ds(low, 8), :]


def near_of(v, swap):
    return jnp.where(swap, pltpu.roll(v, 128 - (HALF - 1), 1), v)


def front_kernel(
    plan, mesh_shape, levels, lab_hbm, pot_hbm, codes_hbm, table_hbm, even, even_near,
    lab, pot, codes, table, lab_up, pot_up, raw, pack, strip, odd, odd_near, even_strip, odd_strip,
    in_sems, g_send, g_recv, y_send, y_recv, z_send, z_recv,
):
    g, y, z = lax.axis_index("grow"), lax.axis_index("gy"), lax.axis_index("gz")
    count_g, count_y, count_z = mesh_shape
    rows, tall, planes, shift = plan.rows, plan.tall, plan.planes, plan.shift
    has_below, has_above = g > 0, g < count_g - 1
    is_first, is_last = g == 0, g == count_g - 1
    y_up, y_down = lax.rem(y + 1, count_y), lax.rem(y + count_y - 1, count_y)
    z_other = lax.rem(z + 1, count_z)
    chunks = plan.chunks
    own_chunks = (planes - plan.low) // 8
    lead = (planes - plan.low) % 8

    loads = [
        pltpu.make_async_copy(lab_hbm, lab, in_sems.at[0]),
        pltpu.make_async_copy(pot_hbm, pot, in_sems.at[1]),
    ]
    melt_loads = [
        pltpu.make_async_copy(codes_hbm, codes, in_sems.at[2]),
        pltpu.make_async_copy(table_hbm, table, in_sems.at[3]),
    ]
    for copy in loads:
        copy.start()

    @pl.when(is_last)
    def _():
        for copy in melt_loads:
            copy.start()

    barrier = pltpu.get_barrier_semaphore()

    def greet(target):
        pl.semaphore_signal(barrier, inc=1, device_id=target, device_id_type=MESH)

    @pl.when(has_below)
    def _():
        greet((g - 1, y, z))

    @pl.when(has_above)
    def _():
        greet((g + 1, y, z))

    greet((g, y_up, z))
    greet((g, y_down, z))
    greet((g, y, z_other))

    splits = [0] + list(range(8 - lead, plan.above - 1, 8)) + [plan.above]
    pieces = len(splits) - 1

    def g_copies(piece):
        begin, end = splits[piece], splits[piece + 1]
        src, dst = pl.ds(begin * rows, (end - begin) * rows), pl.ds((lead + begin) * rows, (end - begin) * rows)
        copies = []
        for i in range(3):
            source, target = (lab.at[src], lab_up.at[dst]) if i == 0 else (pot.at[i - 1, src], pot_up.at[i - 1, dst])
            sem = 3 * piece + i
            copies.append(pltpu.make_async_remote_copy(
                src_ref=source, dst_ref=target, send_sem=g_send.at[sem], recv_sem=g_recv.at[sem],
                device_id=(g - 1, y, z), device_id_type=MESH))
        return copies

    def y_copies(chunk):
        copies = []
        for up in range(2):
            src, dst, target = (rows, 0, y_up) if up else (STEPS, STEPS + rows, y_down)
            sem = 2 * chunk + up
            at = pl.ds(PAD + 8 * chunk, 8)
            copies.append(pltpu.make_async_remote_copy(
                src_ref=raw.at[:, pl.ds(src, STEPS), at], dst_ref=raw.at[:, pl.ds(dst, STEPS), at],
                send_sem=y_send.at[sem], recv_sem=y_recv.at[sem],
                device_id=(g, target, z), device_id_type=MESH))
        return copies

    def z_copy(chunk):
        at = pl.ds(PAD + 8 * chunk, 8)
        return pltpu.make_async_remote_copy(
            src_ref=pack.at[:, :, at], dst_ref=strip.at[:, :, at],
            send_sem=z_send.at[chunk], recv_sem=z_recv.at[chunk],
            device_id=(g, y, z_other), device_id_type=MESH)

    def fill(labels, pots, begin, to):
        for row in range(rows):
            at = pl.ds(begin * rows + row, 8, stride=rows)
            raw[0, STEPS + row, pl.ds(to, 8)] = labels[at].astype(jnp.float32)
            for i in range(2):
                raw[1 + i, STEPS + row, pl.ds(to, 8)] = pots[i, at]

    def send_y(chunk):
        for copy in y_copies(chunk):
            copy.start()

    lane = lanes()

    def send_z(chunk):
        for copy in y_copies(chunk):
            copy.wait_recv()
        at = pl.ds(PAD + 8 * chunk, 8)

        def pack_field(i, carry):
            for group in range(GROUPS):
                packed = jnp.zeros((8, 128), jnp.float32)
                for slot in range(tall // GROUPS):
                    v = raw[i, GROUPS * slot + group, at]
                    first = SLOT * slot
                    packed = jnp.where(lane >= first, pltpu.roll(v, first + HALF // 2 + 1, 1), packed)
                    packed = jnp.where(lane >= first + HALF, pltpu.roll(v, first + HALF + HALF // 2, 1), packed)
                pack[i, group, at] = packed
            return carry

        lax.fori_loop(0, 3, pack_field, 0)
        z_copy(chunk).start()

    place = lane % SLOT
    from_other = (place < HALF // 2 + 1) | (place >= SLOT - HALF // 2 - 1)
    swap = place == HALF // 2 + 1
    at_left, at_right = lane == 0, lane == 127

    def unpack_row(state, slot, row, source, target):
        at = pl.ds(source, 8)
        new = phase_state(raw[0, row, at], [raw[1, row, at], raw[2, row, at]])
        for f in range(FIELDS):
            state[slot, f, row, pl.ds(target, 8)] = new[f]

    def unpack_strips(state, near, slot, source, target):
        at, to = pl.ds(source, 8), pl.ds(target, 8)
        for group in range(GROUPS):
            value = [jnp.where(from_other, strip[i, group, at], pack[i, group, at]) for i in range(3)]
            new = phase_state(value[0], value[1:])
            for f in range(FIELDS):
                state[slot, f, group, to] = new[f]
            for f in range(MOVING):
                near[slot, f, group, to] = near_of(new[f], swap)

    def unpack(chunk):
        to = PAD + 8 * chunk

        def body(part, carry):
            for row in range(tall // GROUPS):
                unpack_row(even, 0, tall // GROUPS * part + row, to, to)
            return carry

        lax.fori_loop(0, GROUPS, body, 0)
        unpack_strips(even_strip, even_near, 0, to, to)

    def strip_step(src, src_slot, dst, near, dst_slot, low):
        at = pl.ds(low, 8)
        for group in range(GROUPS):
            sums = []
            for f in range(MOVING):
                v = src[src_slot, f, group, at]
                up = src[src_slot, f, (group + 1) % GROUPS, at]
                down = src[src_slot, f, (group + 2) % GROUPS, at]
                if group == 0:
                    down = pltpu.roll(down, SLOT, 1)
                if group == GROUPS - 1:
                    up = pltpu.roll(up, 128 - SLOT, 1)
                total = src[src_slot, f, group, pl.ds(low + 1, 8)] + src[src_slot, f, group, pl.ds(low - 1, 8)]
                sums.append((total + (up + down)) + (pltpu.roll(v, 127, 1) + pltpu.roll(v, 1, 1)))
            new = cell_step(sums, *center(src.at[src_slot], group, low))
            for f in range(FIELDS):
                dst[dst_slot, f, group, at] = new[f]
            for f in range(MOVING):
                near[dst_slot, f, group, at] = near_of(new[f], swap)

    def row_steps(src, src_near, src_slot, dst, dst_slot, low, begin, width, count):
        def body(part, carry):
            for i in range(width):
                row = begin + width * part + i
                sums = main_sums(src.at[src_slot], src_near.at[src_slot], row, low, at_left, at_right)
                new = cell_step(sums, *center(src.at[src_slot], row, low))
                for f in range(FIELDS):
                    dst[dst_slot, f, row, pl.ds(low, 8), :] = new[f]
            return carry

        lax.fori_loop(0, count, body, 0)

    def copy_plane(state, strips, near, slot, source, target):
        src, dst = pl.ds(source, 1), pl.ds(target, 1)

        def body(row, carry):
            for f in range(MOVING):
                state[slot, f, row, dst] = state[slot, f, row, src]
            return carry

        lax.fori_loop(0, tall, body, 0)
        for group in range(GROUPS):
            for f in range(MOVING):
                strips[slot, f, group, dst] = strips[slot, f, group, src]
                near[slot, f, group, dst] = near[slot, f, group, src]

    def melt_fill(low):
        def body(row, carry):
            unpack_row(odd, 1, row, low + 1, low)
            return carry

        lax.fori_loop(STEPS_BEFORE, tall - STEPS_BEFORE, body, 0)
        unpack_strips(odd_strip, odd_near, 1, low + 1, low)

    first_plane, top_plane = plan.at(shift), plan.at(planes)
    last_plane = first_plane + planes - 1

    def stage_of(plane, step):
        return (plane - (PAD + 1 - step)) // 8

    def compute(stage):
        def two_steps(t, carry):
            step = 2 * t + 1
            low = PAD + 1 + 8 * stage - step
            top = stage_of(top_plane, STEPS_BEFORE)
            below_melt = (stage <= top) | jnp.logical_not(is_last)

            @pl.when(below_melt)
            def _():
                strip_step(even_strip, t, odd_strip, odd_near, t, low)
                row_steps(even, even_near, t, odd, t, low, step, 4, 4 - t)

            @pl.when(is_last & (t == 0) & (stage == stage_of(top_plane, 1)))
            def _():
                copy_plane(odd, odd_strip, odd_near, 0, top_plane - 1, top_plane)

            @pl.when(is_first & (t == 1) & (stage == stage_of(first_plane, 3)))
            def _():
                copy_plane(odd, odd_strip, odd_near, 1, first_plane, first_plane - 1)

            @pl.when(is_last & (t == 1) & (stage >= top))
            def _():
                melt_fill(jnp.clip(low, top_plane, top_plane + shift + 1 - 8))

            @pl.when(below_melt | (t == 1))
            def _():
                strip_step(odd_strip, t, even_strip, even_near, t + 1, low - 1)
                row_steps(odd, odd_near, t, even, t + 1, low - 1, step + 1, 5, 3 - t)

            @pl.when(is_last & (t == 0) & (stage == stage_of(top_plane, 2)))
            def _():
                copy_plane(even, even_strip, even_near, 1, top_plane - 1, top_plane)

            @pl.when(is_first & (t == 1) & (stage == stage_of(first_plane, 4)))
            def _():
                copy_plane(even, even_strip, even_near, 2, first_plane, first_plane - 1)

            @pl.when(is_last & (t == 1) & (stage == stage_of(last_plane, 4)))
            def _():
                copy_plane(even, even_strip, even_near, 2, last_plane, last_plane + 1)

            return carry

        lax.fori_loop(0, 2, two_steps, 0)

    for copy in loads:
        copy.wait()

    def fill_own(chunk, carry):
        fill(lab, pot, plan.low - PAD + 8 * chunk, 8 * chunk)
        return carry

    lax.fori_loop(0, own_chunks + 1, fill_own, 0)
    tail = pl.ds((planes - lead) * rows, lead * rows)
    lab_up[0 : lead * rows] = lab[tail]
    for i in range(2):
        pot_up[i, 0 : lead * rows] = pot[i, tail]

    @pl.when(is_last)
    def _():
        for copy in melt_loads:
            copy.wait()
        plane = pl.ds((planes - 1) * rows, rows)
        at = pl.ds(lead * rows, rows)
        lab_up[at] = lab[plane]
        for i in range(2):
            pot_up[i, at] = pot[i, plane]

        def melt_plane(k, carry):
            code = codes[pl.ds(pl.multiple_of(jnp.minimum(k, shift - 1) * rows, rows), rows)]
            at = pl.ds(pl.multiple_of((lead + 1 + k) * rows, rows), rows)
            lab_up[at] = jnp.full((rows, 128), 3, jnp.int32)
            for i in range(2):
                value = jnp.zeros((rows, 128), jnp.float32)
                for level in range(levels):
                    value = jnp.where(code == level, table[i, level], value)
                pot_up[i, at] = value
            return carry

        lax.fori_loop(0, plan.above - 1, melt_plane, 0)

    pl.semaphore_wait(barrier, 3 + has_below.astype(jnp.int32) + has_above.astype(jnp.int32))

    @pl.when(has_below)
    def _():
        for piece in range(pieces):
            for copy in g_copies(piece):
                copy.start()

    def first_sends(chunk, carry):
        send_y(chunk)
        return carry

    lax.fori_loop(0, own_chunks, first_sends, 0)

    def beat(it, carry):
        @pl.when(it < chunks)
        def _():
            send_z(it)

        for piece in range(pieces):
            @pl.when(has_above & (it == piece))
            def _():
                for copy in g_copies(piece):
                    copy.wait_recv()

        @pl.when(it < pieces)
        def _():
            fill(lab_up, pot_up, 8 * it, PAD + 8 * (own_chunks + it))
            send_y(own_chunks + it)

        @pl.when(it == pieces)
        def _():
            fill(lab_up, pot_up, 8 * it, PAD + 8 * (own_chunks + it))

        @pl.when((it >= 1) & (it <= chunks))
        def _():
            z_copy(it - 1).wait_recv()

        unpack(it - 1)

        @pl.when(it >= 2)
        def _():
            compute(it - 2)

        return carry

    lax.fori_loop(0, chunks + 2, beat, 0)

    def drain(chunk, carry):
        for copy in y_copies(chunk):
            copy.wait_send()
        z_copy(chunk).wait_send()
        return carry

    lax.fori_loop(0, chunks, drain, 0)

    @pl.when(has_below)
    def _():
        for piece in range(pieces):
            for copy in g_copies(piece):
                copy.wait_send()


def last_kernel(plan, state, near, phases, potentials, p_out, m_out, sems):
    rows, planes = plan.rows, plan.planes
    at_left, at_right = lanes() == 0, lanes() == 127
    slot = STEPS // 2

    def out_copies(tile):
        at = pl.ds(8 * tile * rows, 8 * rows)
        return [
            pltpu.make_async_copy(src.at[:, at], dst.at[:, at], sems.at[2 * tile + i])
            for i, (src, dst) in enumerate(((p_out, phases), (m_out, potentials)))
        ]

    def body(tile, carry):
        low = plan.at(plan.shift) + 8 * tile
        for row in range(rows):
            sums = main_sums(state.at[slot], near.at[slot], STEPS + row, low, at_left, at_right)
            p, m = last_step(sums, *center(state.at[slot], STEPS + row, low))
            at = pl.ds(8 * tile * rows + row, 8, stride=rows)
            for f in range(4):
                p_out[f, at, :] = p[f]
            for i in range(2):
                m_out[i, at, :] = m[i]
        for copy in out_copies(tile):
            copy.start()
        return carry

    lax.fori_loop(0, planes // 8, body, 0)
    for tile in range(planes // 8):
        for copy in out_copies(tile):
            copy.wait()


def on_device(mesh_shape, labels, potential, melt_codes, melt_table):
    planes, rows, width = labels.shape
    shift, levels = melt_codes.shape[0], melt_table.shape[1]
    plan = Plan(planes, rows, shift)
    flat = planes * rows
    vmem = pl.BlockSpec(memory_space=pltpu.VMEM)
    hbm = pl.BlockSpec(memory_space=pltpu.HBM)
    f32 = jnp.float32
    dma = pltpu.SemaphoreType.DMA
    deep, tall, chunks = plan.deep, plan.tall, plan.chunks
    evens, odds = STEPS // 2 + 1, STEPS // 2
    upper = 8 * (plan.above // 8 + 2) * rows
    state, near = pl.pallas_call(
        functools.partial(front_kernel, plan, mesh_shape, levels),
        out_shape=(
            pltpu.VMEM((evens, FIELDS, tall, deep, width), f32),
            pltpu.VMEM((evens, MOVING, GROUPS, deep, width), f32),
        ),
        in_specs=[hbm, hbm, hbm, hbm],
        out_specs=(vmem, vmem),
        scratch_shapes=[
            pltpu.VMEM((flat, width), jnp.int32),
            pltpu.VMEM((2, flat, width), f32),
            pltpu.VMEM((shift * rows, width), jnp.int32),
            pltpu.SMEM((2, levels), f32),
            pltpu.VMEM((upper, width), jnp.int32),
            pltpu.VMEM((2, upper, width), f32),
            pltpu.VMEM((3, tall, deep, width), f32),
            pltpu.VMEM((3, GROUPS, deep, width), f32),
            pltpu.VMEM((3, GROUPS, deep, width), f32),
            pltpu.VMEM((odds, FIELDS, tall, deep, width), f32),
            pltpu.VMEM((odds, MOVING, GROUPS, deep, width), f32),
            pltpu.VMEM((evens, FIELDS, GROUPS, deep, width), f32),
            pltpu.VMEM((odds, FIELDS, GROUPS, deep, width), f32),
            dma((4,)), dma((3 * chunks,)), dma((3 * chunks,)),
            dma((2 * chunks,)), dma((2 * chunks,)), dma((chunks,)), dma((chunks,)),
        ],
        compiler_params=pltpu.CompilerParams(collective_id=0, has_side_effects=True, vmem_limit_bytes=40 << 20),
        name="front",
    )(labels.reshape(flat, width), potential.reshape(2, flat, width), melt_codes.reshape(shift * rows, width), melt_table)
    state, near = (pltpu.with_memory_space_constraint(v, pltpu.VMEM) for v in (state, near))
    phases, potentials = pl.pallas_call(
        functools.partial(last_kernel, plan),
        out_shape=(
            jax.ShapeDtypeStruct((4, flat, width), f32),
            jax.ShapeDtypeStruct((2, flat, width), f32),
        ),
        in_specs=[vmem, vmem],
        out_specs=(hbm, hbm),
        scratch_shapes=[
            pltpu.VMEM((4, flat, width), f32),
            pltpu.VMEM((2, flat, width), f32),
            dma((2 * (planes // 8),)),
        ],
        compiler_params=pltpu.CompilerParams(vmem_limit_bytes=8 << 20),
        name="last",
    )(state, near)
    return phases.reshape(4, planes, rows, width), potentials.reshape(2, planes, rows, width)


def solution(mesh):
    mesh_shape = tuple(mesh.shape[axis] for axis in ("grow", "gy", "gz"))
    return jax.shard_map(
        functools.partial(on_device, mesh_shape),
        mesh=mesh,
        in_specs=(P("grow", "gy", "gz"), P(None, "grow", "gy", "gz"), P(None, "gy", "gz"), P()),
        out_specs=(P(None, "grow", "gy", "gz"), P(None, "grow", "gy", "gz")),
        check_vma=False,
    )
```

time: 40.9 us -> 34.9 us (0.85)
  Pallas kernels: 38.4 us -> 34.1 us
  local copies, waits for them, and re-layouts: 1.51 us -> 0 us
    pallas_call x1, Pallas kernels: 8.63 us -> 1.69 us  [on_device(): pl.pallas_call(functools.partial(last_kernel, plan), out_shape=(jax.Shape...]
    pallas_call x1, Pallas kernels: 29.8 us -> 32.4 us  [on_device(): pl.pallas_call(functools.partial(front_kernel, plan, mesh_shape, levels),...]
    unnamed x4 -> x0, local copies, waits for them, and re-layouts: 1.51 us -> none
where the time goes in v2:
time: 34.9 us; the launch traced here: 34.8 us
  Pallas kernels  34.1 us (98%)
  between operations  0.64 us (2%)
    pallas_call x1, Pallas kernels, on_device(): pl.pallas_call(functools.partial(front_kernel, plan, mesh_shape, levels),...  32.4 us
    pallas_call x1, Pallas kernels, on_device(): pl.pallas_call(functools.partial(last_kernel, plan), out_shape=(jax.Shape...  1.69 us

profile of v2, /device:TPU:0, one launch (start us, length us, event | category | flops | bytes accessed | tf_op | source)
XLA Modules:
  0.0 34.8 jit_solution(14315793420187084507)
XLA Ops:
  0.6 32.4 %front.1 = (f32[3,11,18,56,128]{4,3,2,1,0:T(8,128)S(1)}, f32[3,5,3,56,128]{4,3,2,1,0:T(8,128)S(1)}) custom-call(s32[256,128]{1,0:T(8,128)} %bitcast.6, f32[2,256,128]{2,1,0:T(8,128)} %bitcast.5, s32[128,128]{1,0:T(8,128)} %bitcast.7, f32[2,8]{1,0:T(2,128)} %table_hbm.1), custom_call_target="tpu_custom_call" | custom-call | tf_op jit(solution)/shard_map/front/pallas_call | solution.py:515
  33.1 1.7 %last.1 = (f32[4,256,128]{2,1,0:T(8,128)}, f32[2,256,128]{2,1,0:T(8,128)}) custom-call(f32[3,11,18,56,128]{4,3,2,1,0:T(8,128)S(1)} %get-tuple-element.6.state, f32[3,5,3,56,128]{4,3,2,1,0:T(8,128)S(1)} %get-tuple-element.7.near), custom_call_target="tpu_custom_call" | custom-call | tf_op jit(solution)/shard_map/last/pallas_call | solution.py:544

commit v3 on v2

--- a/solution.py
+++ b/solution.py
@@ -13,9 +13,10 @@
 HALF = 9
 SLOT = 2 * HALF
 GROUPS = 3
+BATCH = 6
 FIELDS = 11
 MOVING = 5
-PAD = 8
+VMEM_BYTES = 67043328
 MESH = pl.DeviceIdType.MESH
 
 LAM = 0.12
@@ -29,14 +30,20 @@
 class Plan:
     def __init__(self, planes, rows, shift):
         self.planes, self.rows, self.shift = planes, rows, shift
-        self.low = shift - STEPS + 1
-        self.chunks = planes // 8 + 1
-        self.deep = 8 * (self.chunks + 2)
+        self.base = shift - STEPS + 2 - 8
+        self.chunks = planes // 8 + 2
+        self.stages = self.chunks - 1
+        self.deep = 8 * self.chunks
         self.above = shift + STEPS
         self.tall = rows + 2 * STEPS
+        self.own_chunks, self.lead = divmod(planes - self.base, 8)
+        self.pieces = self.chunks - self.own_chunks
 
     def at(self, plane):
-        return plane - self.low + PAD
+        return plane - self.base
+
+    def low(self, stage, step):
+        return 8 + 8 * stage - step
 
 
 def phase_state(label, pot):
@@ -57,25 +64,40 @@
     return held, 1.0 / ((held[0] + held[1]) + (held[2] + held[3]))
 
 
-def cell_step(sums, y, rest, mob):
+def cell_step(sums, y, rest, mob, tick=lambda: None):
     held, inverse = clip_step(sums, y)
+    tick()
     total = [rest[i] + mob * sums[3 + i] for i in range(2)]
+    tick()
     scaled = LAM * inverse
     q = [v * scaled for v in held]
+    tick()
     square = [v * v for v in q]
+    tick()
     h = [square[a] * (1.5 * LAM - q[a]) for a in range(4)]
+    tick()
     shared = BACK * ((h[0] + h[1]) + (h[2] + 3.5 * h[3]))
+    tick()
     u = [(total[i] - shared) - (7.0 * BACK) * h[i] for i in range(2)]
+    tick()
     both = u[0] + u[1]
+    well = OWN - ((square[0] + square[1]) + (square[2] + square[3]))
+    tick()
     third = both * (1.0 / 7.0) + TILT
     pull = [third + u[0], third + u[1], third, 0.5 * both]
-    well = OWN - ((square[0] + square[1]) + (square[2] + square[3]))
-    local = [q[a] * ((well + square[a]) + pull[a] * (LAM - q[a])) for a in range(4)]
-    mean = 0.25 * ((local[0] + local[1]) + (local[2] + local[3])) - 0.07 / BETA
-    y = [BETA * (local[a] - mean) for a in range(3)]
+    tick()
     mob = 0.0075 + (0.1425 / LAM) * q[3]
     six = 6.0 * mob
     rest = [total[i] - six * u[i] for i in range(2)]
+    tick()
+    local = []
+    for a in range(4):
+        local.append(q[a] * ((well + square[a]) + pull[a] * (LAM - q[a])))
+        tick()
+    mean = 0.25 * ((local[0] + local[1]) + (local[2] + local[3])) - 0.07 / BETA
+    tick()
+    y = [BETA * (local[a] - mean) for a in range(3)]
+    tick()
     return q[:3] + u + y + rest + [mob]
 
 
@@ -92,8 +114,9 @@
     return lax.broadcasted_iota(jnp.int32, (8, 128), 1)
 
 
-def main_sums(state, near, row, low, at_left, at_right):
-    slot, group = (row // GROUPS, row % GROUPS) if isinstance(row, int) else (lax.div(row, GROUPS), lax.rem(row, GROUPS))
+def side_sums(state, near, row, low, at_left, at_right, first=0):
+    slot = (row + first) // GROUPS if isinstance(row, int) else lax.shift_right_logical(row * 43, 7)
+    group = row + first - GROUPS * slot
     turn = 128 - (SLOT * slot + HALF // 2 + 1)
     sums = []
     for f in range(MOVING):
@@ -101,9 +124,16 @@
         edge = pltpu.roll(near[f, group, pl.ds(low, 8), :], turn, 1)
         right = pltpu.roll(jnp.where(at_left, edge, v), 127, 1)
         left = pltpu.roll(jnp.where(at_right, edge, v), 1, 1)
+        sums.append(right + left)
+    return sums
+
+
+def main_sums(state, row, low, sides):
+    sums = []
+    for f in range(MOVING):
         grow = state[f, row, pl.ds(low + 1, 8), :] + state[f, row, pl.ds(low - 1, 8), :]
         side = state[f, row + 1, pl.ds(low, 8), :] + state[f, row - 1, pl.ds(low, 8), :]
-        sums.append((grow + side) + (right + left))
+        sums.append((grow + side) + sides[f])
     return sums
 
 
@@ -118,8 +148,8 @@
 
 
 def front_kernel(
-    plan, mesh_shape, levels, lab_hbm, pot_hbm, codes_hbm, table_hbm, even, even_near,
-    lab, pot, codes, table, lab_up, pot_up, raw, pack, strip, odd, odd_near, even_strip, odd_strip,
+    plan, mesh_shape, levels, lab_hbm, pot_hbm, codes_hbm, table_hbm, out_state, out_near,
+    lab, pot, codes, table, lab_up, pot_up, raw, pack, strip, even, odd, even_near, odd_near, even_strip, odd_strip,
     in_sems, g_send, g_recv, y_send, y_recv, z_send, z_recv,
 ):
     g, y, z = lax.axis_index("grow"), lax.axis_index("gy"), lax.axis_index("gz")
@@ -130,8 +160,7 @@
     y_up, y_down = lax.rem(y + 1, count_y), lax.rem(y + count_y - 1, count_y)
     z_other = lax.rem(z + 1, count_z)
     chunks = plan.chunks
-    own_chunks = (planes - plan.low) // 8
-    lead = (planes - plan.low) % 8
+    own_chunks, lead, pieces = plan.own_chunks, plan.lead, plan.pieces
 
     loads = [
         pltpu.make_async_copy(lab_hbm, lab, in_sems.at[0]),
@@ -166,15 +195,14 @@
     greet((g, y_down, z))
     greet((g, y, z_other))
 
-    splits = [0] + list(range(8 - lead, plan.above - 1, 8)) + [plan.above]
-    pieces = len(splits) - 1
+    splits = [max(8 * piece - lead, 0) for piece in range(pieces + 1)]
 
     def g_copies(piece):
         begin, end = splits[piece], splits[piece + 1]
         src, dst = pl.ds(begin * rows, (end - begin) * rows), pl.ds((lead + begin) * rows, (end - begin) * rows)
         copies = []
         for i in range(3):
-            source, target = (lab.at[src], lab_up.at[dst]) if i == 0 else (pot.at[i - 1, src], pot_up.at[i - 1, dst])
+            source, target = (lab_hbm.at[src], lab_up.at[dst]) if i == 0 else (pot_hbm.at[i - 1, src], pot_up.at[i - 1, dst])
             sem = 3 * piece + i
             copies.append(pltpu.make_async_remote_copy(
                 src_ref=source, dst_ref=target, send_sem=g_send.at[sem], recv_sem=g_recv.at[sem],
@@ -186,7 +214,7 @@
         for up in range(2):
             src, dst, target = (rows, 0, y_up) if up else (STEPS, STEPS + rows, y_down)
             sem = 2 * chunk + up
-            at = pl.ds(PAD + 8 * chunk, 8)
+            at = pl.ds(8 * chunk, 8)
             copies.append(pltpu.make_async_remote_copy(
                 src_ref=raw.at[:, pl.ds(src, STEPS), at], dst_ref=raw.at[:, pl.ds(dst, STEPS), at],
                 send_sem=y_send.at[sem], recv_sem=y_recv.at[sem],
@@ -194,7 +222,7 @@
         return copies
 
     def z_copy(chunk):
-        at = pl.ds(PAD + 8 * chunk, 8)
+        at = pl.ds(8 * chunk, 8)
         return pltpu.make_async_remote_copy(
             src_ref=pack.at[:, :, at], dst_ref=strip.at[:, :, at],
             send_sem=z_send.at[chunk], recv_sem=z_recv.at[chunk],
@@ -216,7 +244,7 @@
     def send_z(chunk):
         for copy in y_copies(chunk):
             copy.wait_recv()
-        at = pl.ds(PAD + 8 * chunk, 8)
+        at = pl.ds(8 * chunk, 8)
 
         def pack_field(i, carry):
             for group in range(GROUPS):
@@ -254,7 +282,7 @@
                 near[slot, f, group, to] = near_of(new[f], swap)
 
     def unpack(chunk):
-        to = PAD + 8 * chunk
+        to = 8 * chunk
 
         def body(part, carry):
             for row in range(tall // GROUPS):
@@ -264,37 +292,93 @@
         lax.fori_loop(0, GROUPS, body, 0)
         unpack_strips(even_strip, even_near, 0, to, to)
 
-    def strip_step(src, src_slot, dst, near, dst_slot, low):
+    def strip_step(src, src_slot, dst, near, dst_slot, low, tick):
         at = pl.ds(low, 8)
-        for group in range(GROUPS):
+        groups = range(GROUPS)
+        sums = []
+        for f in range(MOVING):
+            v = src[src_slot, f, :, at]
+            part = [src[src_slot, f, group, at] for group in groups]
+            up = jnp.stack([part[1], part[2], pltpu.roll(part[0], 128 - SLOT, 1)])
+            down = jnp.stack([pltpu.roll(part[2], SLOT, 1), part[0], part[1]])
+            total = src[src_slot, f, :, pl.ds(low + 1, 8)] + src[src_slot, f, :, pl.ds(low - 1, 8)]
+            sums.append((total + (up + down)) + (pltpu.roll(v, 127, 2) + pltpu.roll(v, 1, 2)))
+        y = [src[src_slot, MOVING + a, :, at] for a in range(3)]
+        rest = [src[src_slot, MOVING + 3 + i, :, at] for i in range(2)]
+        new = cell_step(sums, y, rest, src[src_slot, FIELDS - 1, :, at], tick)
+        for f in range(FIELDS):
+            dst[dst_slot, f, :, at] = new[f]
+        for f in range(MOVING):
+            near[dst_slot, f, :, at] = jnp.where(swap, pltpu.roll(new[f], 128 - (HALF - 1), 2), new[f])
+
+    def side_steps(state, near, first, count, low, result):
+        v, edge, ends = {}, {}, {}
+
+        def near_rolls(f):
+            rolled = []
+            for i in range(count):
+                slot, group = divmod(first + i, GROUPS)
+                rolled.append(pltpu.roll(near[f, group, pl.ds(low, 8), :], 128 - (SLOT * slot + HALF // 2 + 1), 1))
+            edge[f] = jnp.stack(rolled)
+            v[f] = state[f, first : first + count, pl.ds(low, 8), :]
+
+        def z_rolls(f):
+            right = pltpu.roll(jnp.where(at_left, edge[f], v[f]), 127, 2)
+            left = pltpu.roll(jnp.where(at_right, edge[f], v[f]), 1, 2)
+            ends[f] = (right, left)
+
+        def add(f):
+            result[f] = ends[f][0] + ends[f][1]
+
+        pieces = []
+        for f in range(MOVING + 2):
+            if f < MOVING:
+                pieces.append(functools.partial(near_rolls, f))
+            if f >= 1 and f - 1 < MOVING:
+                pieces.append(functools.partial(z_rolls, f - 1))
+            if f >= 2:
+                pieces.append(functools.partial(add, f - 2))
+        return pieces
+
+    def row_steps(src, src_near, src_slot, dst, dst_slot, low, begin, total, strips_first):
+        state, near = src.at[src_slot], src_near.at[src_slot]
+        sizes = [BATCH] * (total // BATCH) + ([total % BATCH] if total % BATCH else [])
+        at = pl.ds(low, 8)
+        ready = {}
+        pending = side_steps(state, near, begin, sizes[0], low, ready)
+
+        def tick():
+            if pending:
+                pending.pop(0)()
+
+        def flush():
+            while pending:
+                pending.pop(0)()
+
+        strips_first(tick)
+        flush()
+        row = begin
+        for k, size in enumerate(sizes):
+            around, ready = ready, {}
+            if k + 1 < len(sizes):
+                pending = side_steps(state, near, row + size, sizes[k + 1], low, ready)
+
+            def rows_of(f, shift=0, step=0):
+                return state[f, row + shift : row + shift + size, pl.ds(low + step, 8), :]
+
             sums = []
             for f in range(MOVING):
-                v = src[src_slot, f, group, at]
-                up = src[src_slot, f, (group + 1) % GROUPS, at]
-                down = src[src_slot, f, (group + 2) % GROUPS, at]
-                if group == 0:
-                    down = pltpu.roll(down, SLOT, 1)
-                if group == GROUPS - 1:
-                    up = pltpu.roll(up, 128 - SLOT, 1)
-                total = src[src_slot, f, group, pl.ds(low + 1, 8)] + src[src_slot, f, group, pl.ds(low - 1, 8)]
-                sums.append((total + (up + down)) + (pltpu.roll(v, 127, 1) + pltpu.roll(v, 1, 1)))
-            new = cell_step(sums, *center(src.at[src_slot], group, low))
+                grow = rows_of(f, 0, 1) + rows_of(f, 0, -1)
+                side = rows_of(f, 1) + rows_of(f, -1)
+                sums.append((grow + side) + around[f])
+                tick()
+            y = [rows_of(MOVING + a) for a in range(3)]
+            rest = [rows_of(MOVING + 3 + i) for i in range(2)]
+            new = cell_step(sums, y, rest, rows_of(FIELDS - 1), tick)
+            flush()
             for f in range(FIELDS):
-                dst[dst_slot, f, group, at] = new[f]
-            for f in range(MOVING):
-                near[dst_slot, f, group, at] = near_of(new[f], swap)
-
-    def row_steps(src, src_near, src_slot, dst, dst_slot, low, begin, width, count):
-        def body(part, carry):
-            for i in range(width):
-                row = begin + width * part + i
-                sums = main_sums(src.at[src_slot], src_near.at[src_slot], row, low, at_left, at_right)
-                new = cell_step(sums, *center(src.at[src_slot], row, low))
-                for f in range(FIELDS):
-                    dst[dst_slot, f, row, pl.ds(low, 8), :] = new[f]
-            return carry
-
-        lax.fori_loop(0, count, body, 0)
+                dst[dst_slot, f, row : row + size, at, :] = new[f]
+            row += size
 
     def copy_plane(state, strips, near, slot, source, target):
         src, dst = pl.ds(source, 1), pl.ds(target, 1)
@@ -310,73 +394,101 @@
                 strips[slot, f, group, dst] = strips[slot, f, group, src]
                 near[slot, f, group, dst] = near[slot, f, group, src]
 
-    def melt_fill(low):
-        def body(row, carry):
-            unpack_row(odd, 1, row, low + 1, low)
-            return carry
-
-        lax.fori_loop(STEPS_BEFORE, tall - STEPS_BEFORE, body, 0)
-        unpack_strips(odd_strip, odd_near, 1, low + 1, low)
-
     first_plane, top_plane = plan.at(shift), plan.at(planes)
     last_plane = first_plane + planes - 1
+    place_up = lax.broadcasted_iota(jnp.int32, (8, 128), 0)
+
+    def melt_fill(stage):
+        source, target = 8 * stage + 8, 8 * stage + 7
+        melt = place_up >= top_plane - target
+        at, to = pl.ds(source, 8), pl.ds(target, 8)
+
+        def body(row, carry):
+            new = phase_state(raw[0, row, at], [raw[1, row, at], raw[2, row, at]])
+            for f in range(FIELDS):
+                pltpu.store(odd.at[1, f, row, to], new[f], mask=melt)
+            return carry
+
+        lax.fori_loop(STEPS_BEFORE, tall - STEPS_BEFORE, body, 0)
+        for group in range(GROUPS):
+            value = [jnp.where(from_other, strip[i, group, at], pack[i, group, at]) for i in range(3)]
+            new = phase_state(value[0], value[1:])
+            for f in range(FIELDS):
+                pltpu.store(odd_strip.at[1, f, group, to], new[f], mask=melt)
+            for f in range(MOVING):
+                pltpu.store(odd_near.at[1, f, group, to], near_of(new[f], swap), mask=melt)
 
     def stage_of(plane, step):
-        return (plane - (PAD + 1 - step)) // 8
+        return (plane - plan.low(0, step)) // 8
 
     def compute(stage):
-        def two_steps(t, carry):
-            step = 2 * t + 1
-            low = PAD + 1 + 8 * stage - step
-            top = stage_of(top_plane, STEPS_BEFORE)
-            below_melt = (stage <= top) | jnp.logical_not(is_last)
-
-            @pl.when(below_melt)
-            def _():
-                strip_step(even_strip, t, odd_strip, odd_near, t, low)
-                row_steps(even, even_near, t, odd, t, low, step, 4, 4 - t)
-
-            @pl.when(is_last & (t == 0) & (stage == stage_of(top_plane, 1)))
-            def _():
-                copy_plane(odd, odd_strip, odd_near, 0, top_plane - 1, top_plane)
-
-            @pl.when(is_first & (t == 1) & (stage == stage_of(first_plane, 3)))
-            def _():
-                copy_plane(odd, odd_strip, odd_near, 1, first_plane, first_plane - 1)
-
-            @pl.when(is_last & (t == 1) & (stage >= top))
-            def _():
-                melt_fill(jnp.clip(low, top_plane, top_plane + shift + 1 - 8))
-
-            @pl.when(below_melt | (t == 1))
-            def _():
-                strip_step(odd_strip, t, even_strip, even_near, t + 1, low - 1)
-                row_steps(odd, odd_near, t, even, t + 1, low - 1, step + 1, 5, 3 - t)
-
-            @pl.when(is_last & (t == 0) & (stage == stage_of(top_plane, 2)))
-            def _():
-                copy_plane(even, even_strip, even_near, 1, top_plane - 1, top_plane)
-
-            @pl.when(is_first & (t == 1) & (stage == stage_of(first_plane, 4)))
-            def _():
-                copy_plane(even, even_strip, even_near, 2, first_plane, first_plane - 1)
-
-            @pl.when(is_last & (t == 1) & (stage == stage_of(last_plane, 4)))
-            def _():
-                copy_plane(even, even_strip, even_near, 2, last_plane, last_plane + 1)
-
-            return carry
-
-        lax.fori_loop(0, 2, two_steps, 0)
+        top = stage_of(top_plane, STEPS_BEFORE)
+        below_melt = (stage <= top) | jnp.logical_not(is_last)
+
+        def advance(step):
+            t = step // 2
+            low = plan.low(stage, step)
+            count = tall - 2 * step
+            if step % 2:
+                strips = functools.partial(strip_step, even_strip, t, odd_strip, odd_near, t, low)
+                row_steps(even, even_near, t, odd, t, low, step, count, strips)
+            else:
+                strips = functools.partial(strip_step, odd_strip, t - 1, even_strip, even_near, t, low)
+                row_steps(odd, odd_near, t - 1, even, t, low, step, count, strips)
+
+        for step in range(1, STEPS):
+            out = (odd, odd_strip, odd_near, step // 2) if step % 2 else (even, even_strip, even_near, step // 2)
+
+            if step <= STEPS_BEFORE:
+                pl.when(below_melt)(functools.partial(advance, step))
+            else:
+                advance(step)
+
+            if step < STEPS_BEFORE:
+                @pl.when(is_last & (stage == stage_of(top_plane, step)))
+                def _():
+                    copy_plane(*out, top_plane - 1, top_plane)
+            else:
+                @pl.when(is_first & (stage == stage_of(first_plane, step)))
+                def _():
+                    copy_plane(*out, first_plane, first_plane - 1)
+
+            if step == STEPS_BEFORE:
+                @pl.when(is_last & (stage >= top))
+                def _():
+                    melt_fill(stage)
+
+            if step == STEPS - 1:
+                @pl.when(is_last & (stage == stage_of(last_plane, step)))
+                def _():
+                    copy_plane(*out, last_plane, last_plane + 1)
+
+        at = pl.ds(plan.low(stage, STEPS - 1), 8)
+        for f in range(FIELDS):
+            for row in range(rows + 2):
+                if f < MOVING or 0 < row <= rows:
+                    out_state[f, row, at] = even[STEPS // 2, f, STEPS - 1 + row, at]
+        for f in range(MOVING):
+            for group in range(GROUPS):
+                out_near[f, group, at] = even_near[STEPS // 2, f, group, at]
+
+    pl.semaphore_wait(barrier, 3 + has_below.astype(jnp.int32) + has_above.astype(jnp.int32))
+
+    @pl.when(has_below)
+    def _():
+        for piece in range(pieces):
+            for copy in g_copies(piece):
+                copy.start()
 
     for copy in loads:
         copy.wait()
 
     def fill_own(chunk, carry):
-        fill(lab, pot, plan.low - PAD + 8 * chunk, 8 * chunk)
+        fill(lab, pot, plan.base + 8 * chunk, 8 * chunk)
+        send_y(chunk)
         return carry
 
-    lax.fori_loop(0, own_chunks + 1, fill_own, 0)
+    lax.fori_loop(0, own_chunks, fill_own, 0)
     tail = pl.ds((planes - lead) * rows, lead * rows)
     lab_up[0 : lead * rows] = lab[tail]
     for i in range(2):
@@ -403,21 +515,7 @@
                 pot_up[i, at] = value
             return carry
 
-        lax.fori_loop(0, plan.above - 1, melt_plane, 0)
-
-    pl.semaphore_wait(barrier, 3 + has_below.astype(jnp.int32) + has_above.astype(jnp.int32))
-
-    @pl.when(has_below)
-    def _():
-        for piece in range(pieces):
-            for copy in g_copies(piece):
-                copy.start()
-
-    def first_sends(chunk, carry):
-        send_y(chunk)
-        return carry
-
-    lax.fori_loop(0, own_chunks, first_sends, 0)
+        lax.fori_loop(0, 8 * pieces - lead - 1, melt_plane, 0)
 
     def beat(it, carry):
         @pl.when(it < chunks)
@@ -432,18 +530,13 @@
 
         @pl.when(it < pieces)
         def _():
-            fill(lab_up, pot_up, 8 * it, PAD + 8 * (own_chunks + it))
+            fill(lab_up, pot_up, 8 * it, 8 * (own_chunks + it))
             send_y(own_chunks + it)
 
-        @pl.when(it == pieces)
-        def _():
-            fill(lab_up, pot_up, 8 * it, PAD + 8 * (own_chunks + it))
-
-        @pl.when((it >= 1) & (it <= chunks))
+        @pl.when(it >= 1)
         def _():
             z_copy(it - 1).wait_recv()
-
-        unpack(it - 1)
+            unpack(it - 1)
 
         @pl.when(it >= 2)
         def _():
@@ -451,7 +544,7 @@
 
         return carry
 
-    lax.fori_loop(0, chunks + 2, beat, 0)
+    lax.fori_loop(0, plan.stages + 2, beat, 0)
 
     def drain(chunk, carry):
         for copy in y_copies(chunk):
@@ -471,7 +564,7 @@
 def last_kernel(plan, state, near, phases, potentials, p_out, m_out, sems):
     rows, planes = plan.rows, plan.planes
     at_left, at_right = lanes() == 0, lanes() == 127
-    slot = STEPS // 2
+    begin, tiles = plan.at(plan.shift), planes // 8
 
     def out_copies(tile):
         at = pl.ds(8 * tile * rows, 8 * rows)
@@ -481,11 +574,11 @@
         ]
 
     def body(tile, carry):
-        low = plan.at(plan.shift) + 8 * tile
-        for row in range(rows):
-            sums = main_sums(state.at[slot], near.at[slot], STEPS + row, low, at_left, at_right)
-            p, m = last_step(sums, *center(state.at[slot], STEPS + row, low))
-            at = pl.ds(8 * tile * rows + row, 8, stride=rows)
+        low = begin + 8 * tile
+        for row in range(1, rows + 1):
+            sums = main_sums(state, row, low, side_sums(state, near, row, low, at_left, at_right, STEPS - 1))
+            p, m = last_step(sums, *center(state, row, low))
+            at = pl.ds(8 * tile * rows + row - 1, 8, stride=rows)
             for f in range(4):
                 p_out[f, at, :] = p[f]
             for i in range(2):
@@ -494,8 +587,8 @@
             copy.start()
         return carry
 
-    lax.fori_loop(0, planes // 8, body, 0)
-    for tile in range(planes // 8):
+    lax.fori_loop(0, tiles, body, 0)
+    for tile in range(tiles):
         for copy in out_copies(tile):
             copy.wait()
 
@@ -511,12 +604,13 @@
     dma = pltpu.SemaphoreType.DMA
     deep, tall, chunks = plan.deep, plan.tall, plan.chunks
     evens, odds = STEPS // 2 + 1, STEPS // 2
-    upper = 8 * (plan.above // 8 + 2) * rows
+    upper = 8 * plan.pieces * rows
+    kept = (FIELDS * (rows + 2) + MOVING * GROUPS) * deep * width * 4
     state, near = pl.pallas_call(
         functools.partial(front_kernel, plan, mesh_shape, levels),
         out_shape=(
-            pltpu.VMEM((evens, FIELDS, tall, deep, width), f32),
-            pltpu.VMEM((evens, MOVING, GROUPS, deep, width), f32),
+            pltpu.VMEM((FIELDS, rows + 2, deep, width), f32),
+            pltpu.VMEM((MOVING, GROUPS, deep, width), f32),
         ),
         in_specs=[hbm, hbm, hbm, hbm],
         out_specs=(vmem, vmem),
@@ -530,14 +624,16 @@
             pltpu.VMEM((3, tall, deep, width), f32),
             pltpu.VMEM((3, GROUPS, deep, width), f32),
             pltpu.VMEM((3, GROUPS, deep, width), f32),
+            pltpu.VMEM((evens, FIELDS, tall, deep, width), f32),
             pltpu.VMEM((odds, FIELDS, tall, deep, width), f32),
+            pltpu.VMEM((evens, MOVING, GROUPS, deep, width), f32),
             pltpu.VMEM((odds, MOVING, GROUPS, deep, width), f32),
             pltpu.VMEM((evens, FIELDS, GROUPS, deep, width), f32),
             pltpu.VMEM((odds, FIELDS, GROUPS, deep, width), f32),
             dma((4,)), dma((3 * chunks,)), dma((3 * chunks,)),
             dma((2 * chunks,)), dma((2 * chunks,)), dma((chunks,)), dma((chunks,)),
         ],
-        compiler_params=pltpu.CompilerParams(collective_id=0, has_side_effects=True, vmem_limit_bytes=40 << 20),
+        compiler_params=pltpu.CompilerParams(collective_id=0, has_side_effects=True, vmem_limit_bytes=(VMEM_BYTES - kept) // 4096 * 4096),
         name="front",
     )(labels.reshape(flat, width), potential.reshape(2, flat, width), melt_codes.reshape(shift * rows, width), melt_table)
     state, near = (pltpu.with_memory_space_constraint(v, pltpu.VMEM) for v in (state, near))

time: 34.9 us -> 30.1 us (0.86)
  Pallas kernels: 34.1 us -> 29.3 us
    pallas_call x1, Pallas kernels: 32.4 us -> 27.6 us  [on_device(): pl.pallas_call(functools.partial(front_kernel, plan, mesh_shape, levels),...]
where the time goes in v3:
time: 30.1 us; the launch traced here: 29.9 us
  Pallas kernels  29.3 us (97%)
  between operations  0.64 us (2%)
    pallas_call x1, Pallas kernels, on_device(): pl.pallas_call(functools.partial(front_kernel, plan, mesh_shape, levels),...  27.6 us
    pallas_call x1, Pallas kernels, on_device(): pl.pallas_call(functools.partial(last_kernel, plan), out_shape=(jax.Shape...  1.69 us

profile of v3, /device:TPU:0, one launch (start us, length us, event | category | flops | bytes accessed | tf_op | source)
XLA Modules:
  0.0 29.9 jit_solution(12808436661353156295)
XLA Ops:
  0.6 27.6 %front.1 = (f32[11,10,48,128]{3,2,1,0:T(8,128)S(1)}, f32[5,3,48,128]{3,2,1,0:T(8,128)S(1)}) custom-call(s32[256,128]{1,0:T(8,128)} %bitcast.6, f32[2,256,128]{2,1,0:T(8,128)} %bitcast.5, s32[128,128]{1,0:T(8,128)} %bitcast.7, f32[2,8]{1,0:T(2,128)} %table_hbm.1), custom_call_target="tpu_custom_call" | custom-call | tf_op jit(solution)/shard_map/front/pallas_call | solution.py:609
  28.3 1.7 %last.1 = (f32[4,256,128]{2,1,0:T(8,128)}, f32[2,256,128]{2,1,0:T(8,128)}) custom-call(f32[11,10,48,128]{3,2,1,0:T(8,128)S(1)} %get-tuple-element.6.state, f32[5,3,48,128]{3,2,1,0:T(8,128)S(1)} %get-tuple-element.7.near), custom_call_target="tpu_custom_call" | custom-call | tf_op jit(solution)/shard_map/last/pallas_call | solution.py:640

commit v4 on v3

--- a/solution.py
+++ b/solution.py
@@ -13,7 +13,8 @@
 HALF = 9
 SLOT = 2 * HALF
 GROUPS = 3
-BATCH = 6
+LAG = 5
+BATCH = 8
 FIELDS = 11
 MOVING = 5
 VMEM_BYTES = 67043328
@@ -149,7 +150,7 @@
 
 def front_kernel(
     plan, mesh_shape, levels, lab_hbm, pot_hbm, codes_hbm, table_hbm, out_state, out_near,
-    lab, pot, codes, table, lab_up, pot_up, raw, pack, strip, even, odd, even_near, odd_near, even_strip, odd_strip,
+    lab, pot, codes, table, lab_up, pot_up, raw, pack, strip, even, odd, even_near, odd_near, even_strip, odd_strip, sides, strip_sides,
     in_sems, g_send, g_recv, y_send, y_recv, z_send, z_recv,
 ):
     g, y, z = lax.axis_index("grow"), lax.axis_index("gy"), lax.axis_index("gz")
@@ -285,24 +286,35 @@
         to = 8 * chunk
 
         def body(part, carry):
-            for row in range(tall // GROUPS):
-                unpack_row(even, 0, tall // GROUPS * part + row, to, to)
+            rows_at = pl.ds(tall // GROUPS * part, tall // GROUPS)
+            at = pl.ds(to, 8)
+            new = phase_state(raw[0, rows_at, at], [raw[1, rows_at, at], raw[2, rows_at, at]])
+            for f in range(FIELDS):
+                even[0, f, rows_at, at] = new[f]
             return carry
 
         lax.fori_loop(0, GROUPS, body, 0)
         unpack_strips(even_strip, even_near, 0, to, to)
 
-    def strip_step(src, src_slot, dst, near, dst_slot, low, tick):
+    def strip_side_steps(src, slot, low, result):
         at = pl.ds(low, 8)
-        groups = range(GROUPS)
+
+        def piece(f):
+            v = src[slot, f, :, at]
+            part = [src[slot, f, group, at] for group in range(GROUPS)]
+            up = jnp.stack([part[1], part[2], pltpu.roll(part[0], 128 - SLOT, 1)])
+            down = jnp.stack([pltpu.roll(part[2], SLOT, 1), part[0], part[1]])
+            result[f] = (up + down) + (pltpu.roll(v, 127, 2) + pltpu.roll(v, 1, 2))
+
+        return [functools.partial(piece, f) for f in range(MOVING)]
+
+    def strip_step(src, src_slot, dst, near, dst_slot, low, around, tick):
+        at = pl.ds(low, 8)
         sums = []
         for f in range(MOVING):
-            v = src[src_slot, f, :, at]
-            part = [src[src_slot, f, group, at] for group in groups]
-            up = jnp.stack([part[1], part[2], pltpu.roll(part[0], 128 - SLOT, 1)])
-            down = jnp.stack([pltpu.roll(part[2], SLOT, 1), part[0], part[1]])
             total = src[src_slot, f, :, pl.ds(low + 1, 8)] + src[src_slot, f, :, pl.ds(low - 1, 8)]
-            sums.append((total + (up + down)) + (pltpu.roll(v, 127, 2) + pltpu.roll(v, 1, 2)))
+            sums.append(total + around[f])
+            tick()
         y = [src[src_slot, MOVING + a, :, at] for a in range(3)]
         rest = [src[src_slot, MOVING + 3 + i, :, at] for i in range(2)]
         new = cell_step(sums, y, rest, src[src_slot, FIELDS - 1, :, at], tick)
@@ -331,37 +343,81 @@
             result[f] = ends[f][0] + ends[f][1]
 
         pieces = []
-        for f in range(MOVING + 2):
+        for f in range(MOVING + 2 * LAG):
             if f < MOVING:
                 pieces.append(functools.partial(near_rolls, f))
-            if f >= 1 and f - 1 < MOVING:
-                pieces.append(functools.partial(z_rolls, f - 1))
-            if f >= 2:
-                pieces.append(functools.partial(add, f - 2))
+            if LAG <= f < MOVING + LAG:
+                pieces.append(functools.partial(z_rolls, f - LAG))
+            if f >= 2 * LAG:
+                pieces.append(functools.partial(add, f - 2 * LAG))
         return pieces
 
-    def row_steps(src, src_near, src_slot, dst, dst_slot, low, begin, total, strips_first):
-        state, near = src.at[src_slot], src_near.at[src_slot]
-        sizes = [BATCH] * (total // BATCH) + ([total % BATCH] if total % BATCH else [])
+    class Ahead:
+        def __init__(self, pieces=()):
+            self.pieces = list(pieces)
+
+        def __call__(self):
+            if self.pieces:
+                self.pieces.pop(0)()
+
+        def flush(self):
+            while self.pieces:
+                self()
+
+    def sizes_of(step):
+        total = tall - 2 * step
+        parts = -(-total // BATCH)
+        return [total // parts + (k < total % parts) for k in range(parts)]
+
+    def buffers(step):
+        if step % 2:
+            return odd, odd_near, odd_strip, step // 2
+        return even, even_near, even_strip, step // 2
+
+    def begin_steps(stage, step, around, strip_around):
+        state, near, strips, slot = buffers(step - 1)
+        low = plan.low(stage, step)
+        rows_ahead = side_steps(state.at[slot], near.at[slot], step, sizes_of(step)[0], low, around)
+        return rows_ahead, strip_side_steps(strips, slot, low, strip_around)
+
+    def keep(around, strip_around):
+        for f in range(MOVING):
+            sides[: around[f].shape[0], f] = around[f]
+            strip_sides[f] = strip_around[f]
+
+    def begin(stage, step):
+        around, strip_around = {}, {}
+        rows_ahead, strips_ahead = begin_steps(stage, step, around, strip_around)
+        for piece in strips_ahead + rows_ahead:
+            piece()
+        keep(around, strip_around)
+
+    def row_steps(stage, step):
+        src, src_near, src_strip, slot = buffers(step - 1)
+        dst, dst_near, dst_strip, dst_slot = buffers(step)
+        state, near = src.at[slot], src_near.at[slot]
+        low = plan.low(stage, step)
+        sizes = sizes_of(step)
         at = pl.ds(low, 8)
-        ready = {}
-        pending = side_steps(state, near, begin, sizes[0], low, ready)
-
-        def tick():
-            if pending:
-                pending.pop(0)()
-
-        def flush():
-            while pending:
-                pending.pop(0)()
-
-        strips_first(tick)
-        flush()
-        row = begin
+        ready, strip_ready = {}, {}
+        if step == 1:
+            rows_ahead, strips_ahead = begin_steps(stage, step, ready, strip_ready)
+            Ahead(strips_ahead).flush()
+            ahead = Ahead(rows_ahead)
+        else:
+            ready = {f: sides[: sizes[0], f] for f in range(MOVING)}
+            strip_ready = {f: strip_sides[f] for f in range(MOVING)}
+            ahead = Ahead()
+        strip_step(src_strip, slot, dst_strip, dst_near, dst_slot, low, strip_ready, ahead)
+        ahead.flush()
+        row = step
         for k, size in enumerate(sizes):
-            around, ready = ready, {}
+            around, ready, strip_ready = ready, {}, {}
             if k + 1 < len(sizes):
-                pending = side_steps(state, near, row + size, sizes[k + 1], low, ready)
+                ahead = Ahead(side_steps(state, near, row + size, sizes[k + 1], low, ready))
+            elif step < STEPS - 1:
+                rows_ahead, strips_ahead = begin_steps(stage, step + 1, ready, strip_ready)
+                ahead = Ahead(strips_ahead + rows_ahead)
 
             def rows_of(f, shift=0, step=0):
                 return state[f, row + shift : row + shift + size, pl.ds(low + step, 8), :]
@@ -371,14 +427,16 @@
                 grow = rows_of(f, 0, 1) + rows_of(f, 0, -1)
                 side = rows_of(f, 1) + rows_of(f, -1)
                 sums.append((grow + side) + around[f])
-                tick()
+                ahead()
             y = [rows_of(MOVING + a) for a in range(3)]
             rest = [rows_of(MOVING + 3 + i) for i in range(2)]
-            new = cell_step(sums, y, rest, rows_of(FIELDS - 1), tick)
-            flush()
+            new = cell_step(sums, y, rest, rows_of(FIELDS - 1), ahead)
+            ahead.flush()
             for f in range(FIELDS):
                 dst[dst_slot, f, row : row + size, at, :] = new[f]
             row += size
+        if step < STEPS - 1:
+            keep(ready, strip_ready)
 
     def copy_plane(state, strips, near, slot, source, target):
         src, dst = pl.ds(source, 1), pl.ds(target, 1)
@@ -425,24 +483,13 @@
         top = stage_of(top_plane, STEPS_BEFORE)
         below_melt = (stage <= top) | jnp.logical_not(is_last)
 
-        def advance(step):
-            t = step // 2
-            low = plan.low(stage, step)
-            count = tall - 2 * step
-            if step % 2:
-                strips = functools.partial(strip_step, even_strip, t, odd_strip, odd_near, t, low)
-                row_steps(even, even_near, t, odd, t, low, step, count, strips)
-            else:
-                strips = functools.partial(strip_step, odd_strip, t - 1, even_strip, even_near, t, low)
-                row_steps(odd, odd_near, t - 1, even, t, low, step, count, strips)
-
         for step in range(1, STEPS):
             out = (odd, odd_strip, odd_near, step // 2) if step % 2 else (even, even_strip, even_near, step // 2)
 
             if step <= STEPS_BEFORE:
-                pl.when(below_melt)(functools.partial(advance, step))
+                pl.when(below_melt)(functools.partial(row_steps, stage, step))
             else:
-                advance(step)
+                row_steps(stage, step)
 
             if step < STEPS_BEFORE:
                 @pl.when(is_last & (stage == stage_of(top_plane, step)))
@@ -457,6 +504,7 @@
                 @pl.when(is_last & (stage >= top))
                 def _():
                     melt_fill(stage)
+                    begin(stage, step + 1)
 
             if step == STEPS - 1:
                 @pl.when(is_last & (stage == stage_of(last_plane, step)))
@@ -518,33 +566,46 @@
         lax.fori_loop(0, 8 * pieces - lead - 1, melt_plane, 0)
 
     def beat(it, carry):
-        @pl.when(it < chunks)
+        first_z = jnp.where(it > own_chunks, it - 1, it)
+        last_z = jnp.where(it == own_chunks, it, jnp.where(it == own_chunks + 2, chunks, jnp.where(it > own_chunks + 2, first_z, first_z + 1)))
+
+        def z_body(chunk, carry):
+            send_z(chunk)
+            return carry
+
+        @pl.when((it > own_chunks) & (it == 2 * (pieces - 1)))
         def _():
-            send_z(it)
-
-        for piece in range(pieces):
-            @pl.when(has_above & (it == piece))
-            def _():
-                for copy in g_copies(piece):
-                    copy.wait_recv()
-
-        @pl.when(it < pieces)
+            take(it)
+
+        lax.fori_loop(first_z, last_z, z_body, 0)
+
+        @pl.when((it < 2 * (pieces - 1)) & (lax.rem(it, 2) == 0))
         def _():
-            fill(lab_up, pot_up, 8 * it, 8 * (own_chunks + it))
-            send_y(own_chunks + it)
-
-        @pl.when(it >= 1)
-        def _():
-            z_copy(it - 1).wait_recv()
-            unpack(it - 1)
+            take(it)
 
         @pl.when(it >= 2)
         def _():
-            compute(it - 2)
+            z_copy(it - 2).wait_recv()
+            unpack(it - 2)
+
+        @pl.when(it >= 3)
+        def _():
+            compute(it - 3)
 
         return carry
 
-    lax.fori_loop(0, plan.stages + 2, beat, 0)
+    def take(it):
+        piece = lax.div(it, 2)
+        for k in range(pieces):
+            @pl.when(has_above & (piece == k))
+            def _():
+                for copy in g_copies(k):
+                    copy.wait_recv()
+
+        fill(lab_up, pot_up, 8 * piece, 8 * (own_chunks + piece))
+        send_y(own_chunks + piece)
+
+    lax.fori_loop(0, plan.stages + 3, beat, 0)
 
     def drain(chunk, carry):
         for copy in y_copies(chunk):
@@ -630,6 +691,8 @@
             pltpu.VMEM((odds, MOVING, GROUPS, deep, width), f32),
             pltpu.VMEM((evens, FIELDS, GROUPS, deep, width), f32),
             pltpu.VMEM((odds, FIELDS, GROUPS, deep, width), f32),
+            pltpu.VMEM((BATCH, MOVING, 8, width), f32),
+            pltpu.VMEM((MOVING, GROUPS, 8, width), f32),
             dma((4,)), dma((3 * chunks,)), dma((3 * chunks,)),
             dma((2 * chunks,)), dma((2 * chunks,)), dma((chunks,)), dma((chunks,)),
         ],

time: 30.1 us -> 27.9 us (0.927)
  Pallas kernels: 29.3 us -> 27.1 us
    pallas_call x1, Pallas kernels: 27.6 us -> 25.4 us  [on_device(): pl.pallas_call(functools.partial(front_kernel, plan, mesh_shape, levels),...]
where the time goes in v4:
time: 27.9 us; the launch traced here: 27.8 us
  Pallas kernels  27.1 us (97%)
  between operations  0.64 us (2%)
    pallas_call x1, Pallas kernels, on_device(): pl.pallas_call(functools.partial(front_kernel, plan, mesh_shape, levels),...  25.4 us
    pallas_call x1, Pallas kernels, on_device(): pl.pallas_call(functools.partial(last_kernel, plan), out_shape=(jax.Shape...  1.69 us

profile of v4, /device:TPU:0, one launch (start us, length us, event | category | flops | bytes accessed | tf_op | source)
XLA Modules:
  0.0 27.8 jit_solution(7295621465811128745)
XLA Ops:
  0.6 25.4 %front.1 = (f32[11,10,48,128]{3,2,1,0:T(8,128)S(1)}, f32[5,3,48,128]{3,2,1,0:T(8,128)S(1)}) custom-call(s32[256,128]{1,0:T(8,128)} %bitcast.6, f32[2,256,128]{2,1,0:T(8,128)} %bitcast.5, s32[128,128]{1,0:T(8,128)} %bitcast.7, f32[2,8]{1,0:T(2,128)} %table_hbm.1), custom_call_target="tpu_custom_call" | custom-call | tf_op jit(solution)/shard_map/front/pallas_call | solution.py:670
  26.1 1.7 %last.1 = (f32[4,256,128]{2,1,0:T(8,128)}, f32[2,256,128]{2,1,0:T(8,128)}) custom-call(f32[11,10,48,128]{3,2,1,0:T(8,128)S(1)} %get-tuple-element.6.state, f32[5,3,48,128]{3,2,1,0:T(8,128)S(1)} %get-tuple-element.7.near), custom_call_target="tpu_custom_call" | custom-call | tf_op jit(solution)/shard_map/last/pallas_call | solution.py:703

commit v5 on v4

--- a/solution.py
+++ b/solution.py
@@ -17,6 +17,8 @@
 BATCH = 8
 FIELDS = 11
 MOVING = 5
+CODE = 16.0
+CODED_AT = (0,) + tuple(range(3, FIELDS))
 VMEM_BYTES = 67043328
 MESH = pl.DeviceIdType.MESH
 
@@ -47,8 +49,11 @@
         return 8 + 8 * stage - step
 
 
-def phase_state(label, pot):
-    q = [jnp.where(label == float(a), LAM, 0.0) for a in range(3)]
+def phase_state(label, pot, coded=False):
+    if coded:
+        q = [jnp.where(label == 0.0, 1.0, jnp.where(label == 1.0, CODE, jnp.where(label == 2.0, CODE * CODE, 0.0)))]
+    else:
+        q = [jnp.where(label == float(a), LAM, 0.0) for a in range(3)]
     y = [jnp.where(label == float(a), LAM * BETA * OWN, 0.0) for a in range(3)]
     liquid = label == 3.0
     mob = jnp.where(liquid, 0.15, 0.0075)
@@ -56,6 +61,17 @@
     comp = [jnp.where(liquid, 0.35 * MU, jnp.where(label == float(i), 0.8 * MU, 0.1 * MU)) for i in range(2)]
     rest = [(u[i] + comp[i]) - (6.0 * mob) * u[i] for i in range(2)]
     return q + u + y + rest + [mob]
+
+
+def decode(total):
+    third = jnp.floor(total * (1.0 / (CODE * CODE)))
+    total = total - (CODE * CODE) * third
+    second = jnp.floor(total * (1.0 / CODE))
+    return [LAM * v for v in (total - CODE * second, second, third)]
+
+
+def moving_of(step):
+    return (0, 3, 4) if step == 1 else tuple(range(MOVING))
 
 
 def clip_step(sums, y):
@@ -210,12 +226,19 @@
                 device_id=(g - 1, y, z), device_id_type=MESH))
         return copies
 
+    def planes_of(chunk):
+        return pl.ds(7, 1) if isinstance(chunk, int) and chunk == 0 else pl.ds(8 * chunk, 8)
+
+    def either(chunk, action):
+        pl.when(chunk == 0)(lambda: action(0))
+        pl.when(chunk > 0)(lambda: action(chunk))
+
     def y_copies(chunk):
         copies = []
         for up in range(2):
             src, dst, target = (rows, 0, y_up) if up else (STEPS, STEPS + rows, y_down)
             sem = 2 * chunk + up
-            at = pl.ds(8 * chunk, 8)
+            at = planes_of(chunk)
             copies.append(pltpu.make_async_remote_copy(
                 src_ref=raw.at[:, pl.ds(src, STEPS), at], dst_ref=raw.at[:, pl.ds(dst, STEPS), at],
                 send_sem=y_send.at[sem], recv_sem=y_recv.at[sem],
@@ -223,7 +246,7 @@
         return copies
 
     def z_copy(chunk):
-        at = pl.ds(8 * chunk, 8)
+        at = planes_of(chunk)
         return pltpu.make_async_remote_copy(
             src_ref=pack.at[:, :, at], dst_ref=strip.at[:, :, at],
             send_sem=z_send.at[chunk], recv_sem=z_recv.at[chunk],
@@ -243,8 +266,7 @@
     lane = lanes()
 
     def send_z(chunk):
-        for copy in y_copies(chunk):
-            copy.wait_recv()
+        either(chunk, lambda k: [copy.wait_recv() for copy in y_copies(k)] and None)
         at = pl.ds(8 * chunk, 8)
 
         def pack_field(i, carry):
@@ -259,7 +281,7 @@
             return carry
 
         lax.fori_loop(0, 3, pack_field, 0)
-        z_copy(chunk).start()
+        either(chunk, lambda k: z_copy(k).start())
 
     place = lane % SLOT
     from_other = (place < HALF // 2 + 1) | (place >= SLOT - HALF // 2 - 1)
@@ -276,11 +298,10 @@
         at, to = pl.ds(source, 8), pl.ds(target, 8)
         for group in range(GROUPS):
             value = [jnp.where(from_other, strip[i, group, at], pack[i, group, at]) for i in range(3)]
-            new = phase_state(value[0], value[1:])
-            for f in range(FIELDS):
-                state[slot, f, group, to] = new[f]
-            for f in range(MOVING):
-                near[slot, f, group, to] = near_of(new[f], swap)
+            for f, v in zip(CODED_AT, phase_state(value[0], value[1:], True)):
+                state[slot, f, group, to] = v
+                if f < MOVING:
+                    near[slot, f, group, to] = near_of(v, swap)
 
     def unpack(chunk):
         to = 8 * chunk
@@ -288,15 +309,15 @@
         def body(part, carry):
             rows_at = pl.ds(tall // GROUPS * part, tall // GROUPS)
             at = pl.ds(to, 8)
-            new = phase_state(raw[0, rows_at, at], [raw[1, rows_at, at], raw[2, rows_at, at]])
-            for f in range(FIELDS):
-                even[0, f, rows_at, at] = new[f]
+            new = phase_state(raw[0, rows_at, at], [raw[1, rows_at, at], raw[2, rows_at, at]], True)
+            for f, v in zip(CODED_AT, new):
+                even[0, f, rows_at, at] = v
             return carry
 
         lax.fori_loop(0, GROUPS, body, 0)
         unpack_strips(even_strip, even_near, 0, to, to)
 
-    def strip_side_steps(src, slot, low, result):
+    def strip_side_steps(fields, src, slot, low, result):
         at = pl.ds(low, 8)
 
         def piece(f):
@@ -306,15 +327,17 @@
             down = jnp.stack([pltpu.roll(part[2], SLOT, 1), part[0], part[1]])
             result[f] = (up + down) + (pltpu.roll(v, 127, 2) + pltpu.roll(v, 1, 2))
 
-        return [functools.partial(piece, f) for f in range(MOVING)]
-
-    def strip_step(src, src_slot, dst, near, dst_slot, low, around, tick):
+        return [functools.partial(piece, f) for f in fields]
+
+    def strip_step(step, src, src_slot, dst, near, dst_slot, low, around, tick):
         at = pl.ds(low, 8)
         sums = []
-        for f in range(MOVING):
+        for f in moving_of(step):
             total = src[src_slot, f, :, pl.ds(low + 1, 8)] + src[src_slot, f, :, pl.ds(low - 1, 8)]
             sums.append(total + around[f])
             tick()
+        if step == 1:
+            sums = decode(sums[0]) + sums[1:]
         y = [src[src_slot, MOVING + a, :, at] for a in range(3)]
         rest = [src[src_slot, MOVING + 3 + i, :, at] for i in range(2)]
         new = cell_step(sums, y, rest, src[src_slot, FIELDS - 1, :, at], tick)
@@ -323,7 +346,7 @@
         for f in range(MOVING):
             near[dst_slot, f, :, at] = jnp.where(swap, pltpu.roll(new[f], 128 - (HALF - 1), 2), new[f])
 
-    def side_steps(state, near, first, count, low, result):
+    def side_steps(fields, state, near, first, count, low, result):
         v, edge, ends = {}, {}, {}
 
         def near_rolls(f):
@@ -343,13 +366,13 @@
             result[f] = ends[f][0] + ends[f][1]
 
         pieces = []
-        for f in range(MOVING + 2 * LAG):
-            if f < MOVING:
-                pieces.append(functools.partial(near_rolls, f))
-            if LAG <= f < MOVING + LAG:
-                pieces.append(functools.partial(z_rolls, f - LAG))
-            if f >= 2 * LAG:
-                pieces.append(functools.partial(add, f - 2 * LAG))
+        for k in range(len(fields) + 2 * LAG):
+            if k < len(fields):
+                pieces.append(functools.partial(near_rolls, fields[k]))
+            if LAG <= k < len(fields) + LAG:
+                pieces.append(functools.partial(z_rolls, fields[k - LAG]))
+            if k >= 2 * LAG:
+                pieces.append(functools.partial(add, fields[k - 2 * LAG]))
         return pieces
 
     class Ahead:
@@ -377,11 +400,11 @@
     def begin_steps(stage, step, around, strip_around):
         state, near, strips, slot = buffers(step - 1)
         low = plan.low(stage, step)
-        rows_ahead = side_steps(state.at[slot], near.at[slot], step, sizes_of(step)[0], low, around)
-        return rows_ahead, strip_side_steps(strips, slot, low, strip_around)
+        rows_ahead = side_steps(moving_of(step), state.at[slot], near.at[slot], step, sizes_of(step)[0], low, around)
+        return rows_ahead, strip_side_steps(moving_of(step), strips, slot, low, strip_around)
 
     def keep(around, strip_around):
-        for f in range(MOVING):
+        for f in around:
             sides[: around[f].shape[0], f] = around[f]
             strip_sides[f] = strip_around[f]
 
@@ -405,29 +428,31 @@
             Ahead(strips_ahead).flush()
             ahead = Ahead(rows_ahead)
         else:
-            ready = {f: sides[: sizes[0], f] for f in range(MOVING)}
-            strip_ready = {f: strip_sides[f] for f in range(MOVING)}
+            ready = {f: sides[: sizes[0], f] for f in moving_of(step)}
+            strip_ready = {f: strip_sides[f] for f in moving_of(step)}
             ahead = Ahead()
-        strip_step(src_strip, slot, dst_strip, dst_near, dst_slot, low, strip_ready, ahead)
+        strip_step(step, src_strip, slot, dst_strip, dst_near, dst_slot, low, strip_ready, ahead)
         ahead.flush()
         row = step
         for k, size in enumerate(sizes):
             around, ready, strip_ready = ready, {}, {}
             if k + 1 < len(sizes):
-                ahead = Ahead(side_steps(state, near, row + size, sizes[k + 1], low, ready))
+                ahead = Ahead(side_steps(moving_of(step), state, near, row + size, sizes[k + 1], low, ready))
             elif step < STEPS - 1:
                 rows_ahead, strips_ahead = begin_steps(stage, step + 1, ready, strip_ready)
                 ahead = Ahead(strips_ahead + rows_ahead)
 
-            def rows_of(f, shift=0, step=0):
-                return state[f, row + shift : row + shift + size, pl.ds(low + step, 8), :]
+            def rows_of(f, shift=0, up=0):
+                return state[f, row + shift : row + shift + size, pl.ds(low + up, 8), :]
 
             sums = []
-            for f in range(MOVING):
+            for f in moving_of(step):
                 grow = rows_of(f, 0, 1) + rows_of(f, 0, -1)
                 side = rows_of(f, 1) + rows_of(f, -1)
                 sums.append((grow + side) + around[f])
                 ahead()
+            if step == 1:
+                sums = decode(sums[0]) + sums[1:]
             y = [rows_of(MOVING + a) for a in range(3)]
             rest = [rows_of(MOVING + 3 + i) for i in range(2)]
             new = cell_step(sums, y, rest, rows_of(FIELDS - 1), ahead)
@@ -533,7 +558,7 @@
 
     def fill_own(chunk, carry):
         fill(lab, pot, plan.base + 8 * chunk, 8 * chunk)
-        send_y(chunk)
+        either(chunk, send_y)
         return carry
 
     lax.fori_loop(0, own_chunks, fill_own, 0)
@@ -585,7 +610,7 @@
 
         @pl.when(it >= 2)
         def _():
-            z_copy(it - 2).wait_recv()
+            either(it - 2, lambda k: z_copy(k).wait_recv())
             unpack(it - 2)
 
         @pl.when(it >= 3)
@@ -608,9 +633,12 @@
     lax.fori_loop(0, plan.stages + 3, beat, 0)
 
     def drain(chunk, carry):
-        for copy in y_copies(chunk):
-            copy.wait_send()
-        z_copy(chunk).wait_send()
+        def wait(k):
+            for copy in y_copies(k):
+                copy.wait_send()
+            z_copy(k).wait_send()
+
+        either(chunk, wait)
         return carry
 
     lax.fori_loop(0, chunks, drain, 0)

time: 27.9 us -> 27.3 us (0.978)
  Pallas kernels: 27.1 us -> 26.4 us
    pallas_call x1, Pallas kernels: 25.4 us -> 24.7 us  [on_device(): pl.pallas_call(functools.partial(front_kernel, plan, mesh_shape, levels),...]
where the time goes in v5:
time: 27.3 us; the launch traced here: 27.1 us
  Pallas kernels  26.4 us (97%)
  between operations  0.64 us (2%)
    pallas_call x1, Pallas kernels, on_device(): pl.pallas_call(functools.partial(front_kernel, plan, mesh_shape, levels),...  24.7 us
    pallas_call x1, Pallas kernels, on_device(): pl.pallas_call(functools.partial(last_kernel, plan), out_shape=(jax.Shape...  1.69 us

profile of v5, /device:TPU:0, one launch (start us, length us, event | category | flops | bytes accessed | tf_op | source)
XLA Modules:
  0.0 27.1 jit_solution(16544324041706732159)
XLA Ops:
  0.6 24.7 %front.1 = (f32[11,10,48,128]{3,2,1,0:T(8,128)S(1)}, f32[5,3,48,128]{3,2,1,0:T(8,128)S(1)}) custom-call(s32[256,128]{1,0:T(8,128)} %bitcast.6, f32[2,256,128]{2,1,0:T(8,128)} %bitcast.5, s32[128,128]{1,0:T(8,128)} %bitcast.7, f32[2,8]{1,0:T(2,128)} %table_hbm.1), custom_call_target="tpu_custom_call" | custom-call | tf_op jit(solution)/shard_map/front/pallas_call | solution.py:698
  25.4 1.7 %last.1 = (f32[4,256,128]{2,1,0:T(8,128)}, f32[2,256,128]{2,1,0:T(8,128)}) custom-call(f32[11,10,48,128]{3,2,1,0:T(8,128)S(1)} %get-tuple-element.6.state, f32[5,3,48,128]{3,2,1,0:T(8,128)S(1)} %get-tuple-element.7.near), custom_call_target="tpu_custom_call" | custom-call | tf_op jit(solution)/shard_map/last/pallas_call | solution.py:731

commit v6 on v5

--- a/solution.py
+++ b/solution.py
@@ -131,9 +131,8 @@
     return lax.broadcasted_iota(jnp.int32, (8, 128), 1)
 
 
-def side_sums(state, near, row, low, at_left, at_right, first=0):
-    slot = (row + first) // GROUPS if isinstance(row, int) else lax.shift_right_logical(row * 43, 7)
-    group = row + first - GROUPS * slot
+def side_sums(state, near, row, low, at_left, at_right):
+    slot, group = divmod(row, GROUPS)
     turn = 128 - (SLOT * slot + HALF // 2 + 1)
     sums = []
     for f in range(MOVING):
@@ -166,8 +165,8 @@
 
 def front_kernel(
     plan, mesh_shape, levels, lab_hbm, pot_hbm, codes_hbm, table_hbm, out_state, out_near,
-    lab, pot, codes, table, lab_up, pot_up, raw, pack, strip, even, odd, even_near, odd_near, even_strip, odd_strip, sides, strip_sides,
-    in_sems, g_send, g_recv, y_send, y_recv, z_send, z_recv,
+    lab, pot, codes, table, lab_up, pot_up, raw, pack, strip, across_pack, across, even, odd, even_near, odd_near, even_strip, odd_strip, out_strip, sides, strip_sides,
+    in_sems, g_send, g_recv, y_send, y_recv, z_send, z_recv, a_send, a_recv,
 ):
     g, y, z = lax.axis_index("grow"), lax.axis_index("gy"), lax.axis_index("gz")
     count_g, count_y, count_z = mesh_shape
@@ -211,6 +210,8 @@
     greet((g, y_up, z))
     greet((g, y_down, z))
     greet((g, y, z_other))
+    greet((g, y_up, z_other))
+    greet((g, y_down, z_other))
 
     splits = [max(8 * piece - lead, 0) for piece in range(pieces + 1)]
 
@@ -246,11 +247,22 @@
         return copies
 
     def z_copy(chunk):
-        at = planes_of(chunk)
+        at = pl.ds(8 * chunk, 8)
         return pltpu.make_async_remote_copy(
             src_ref=pack.at[:, :, at], dst_ref=strip.at[:, :, at],
             send_sem=z_send.at[chunk], recv_sem=z_recv.at[chunk],
             device_id=(g, y, z_other), device_id_type=MESH)
+
+    def across_copies(chunk):
+        at = planes_of(chunk)
+        copies = []
+        for k, row in enumerate((y_up, y, y_down)):
+            sem = 3 * chunk + k
+            copies.append(pltpu.make_async_remote_copy(
+                src_ref=across_pack.at[:, :, at], dst_ref=across.at[k, :, :, at],
+                send_sem=a_send.at[sem], recv_sem=a_recv.at[sem],
+                device_id=(g, row, z_other), device_id_type=MESH))
+        return copies
 
     def fill(labels, pots, begin, to):
         for row in range(rows):
@@ -265,23 +277,60 @@
 
     lane = lanes()
 
-    def send_z(chunk):
-        either(chunk, lambda k: [copy.wait_recv() for copy in y_copies(k)] and None)
+    def pack_rows(target, chunk, source):
         at = pl.ds(8 * chunk, 8)
 
         def pack_field(i, carry):
             for group in range(GROUPS):
                 packed = jnp.zeros((8, 128), jnp.float32)
                 for slot in range(tall // GROUPS):
-                    v = raw[i, GROUPS * slot + group, at]
+                    v = raw[i, source(GROUPS * slot + group), at]
                     first = SLOT * slot
                     packed = jnp.where(lane >= first, pltpu.roll(v, first + HALF // 2 + 1, 1), packed)
                     packed = jnp.where(lane >= first + HALF, pltpu.roll(v, first + HALF + HALF // 2, 1), packed)
-                pack[i, group, at] = packed
+                target[i, group, at] = packed
             return carry
 
         lax.fori_loop(0, 3, pack_field, 0)
-        either(chunk, lambda k: z_copy(k).start())
+
+    def row_across(row):
+        return row + rows if row < STEPS else row - rows if row >= STEPS + rows else row
+
+    def start_all(copies):
+        for copy in copies:
+            copy.start()
+
+    def send_across(chunk, carry):
+        pack_rows(across_pack, chunk, row_across)
+        either(chunk, lambda k: start_all(across_copies(k)))
+        return carry
+
+    def wait_all(copies):
+        for copy in copies:
+            copy.wait_recv()
+
+    def send_z(chunk):
+        either(chunk, lambda k: wait_all(y_copies(k)))
+        pack_rows(pack, chunk, lambda row: row)
+
+        @pl.when(chunk >= own_chunks)
+        def _():
+            z_copy(chunk).start()
+
+    def receive_z(chunk):
+        @pl.when(chunk >= own_chunks)
+        def _():
+            z_copy(chunk).wait_recv()
+
+        @pl.when(chunk < own_chunks)
+        def _():
+            either(chunk, lambda k: wait_all(across_copies(k)))
+            at = pl.ds(8 * chunk, 8)
+            for group in range(GROUPS):
+                own, upper = -((group - STEPS) // GROUPS), -((group - STEPS - rows) // GROUPS)
+                for i in range(3):
+                    value = jnp.where(lane >= SLOT * own, across[1, i, group, at], across[0, i, group, at])
+                    strip[i, group, at] = jnp.where(lane >= SLOT * upper, across[2, i, group, at], value)
 
     place = lane % SLOT
     from_other = (place < HALF // 2 + 1) | (place >= SLOT - HALF // 2 - 1)
@@ -393,6 +442,8 @@
         return [total // parts + (k < total % parts) for k in range(parts)]
 
     def buffers(step):
+        if step == STEPS - 1:
+            return out_state, out_near, out_strip, 0
         if step % 2:
             return odd, odd_near, odd_strip, step // 2
         return even, even_near, even_strip, step // 2
@@ -509,7 +560,8 @@
         below_melt = (stage <= top) | jnp.logical_not(is_last)
 
         for step in range(1, STEPS):
-            out = (odd, odd_strip, odd_near, step // 2) if step % 2 else (even, even_strip, even_near, step // 2)
+            state, near, strips, slot = buffers(step)
+            out = (state, strips, near, slot)
 
             if step <= STEPS_BEFORE:
                 pl.when(below_melt)(functools.partial(row_steps, stage, step))
@@ -525,6 +577,9 @@
                 def _():
                     copy_plane(*out, first_plane, first_plane - 1)
 
+            if step == 2:
+                pass_on(stage)
+
             if step == STEPS_BEFORE:
                 @pl.when(is_last & (stage >= top))
                 def _():
@@ -536,16 +591,7 @@
                 def _():
                     copy_plane(*out, last_plane, last_plane + 1)
 
-        at = pl.ds(plan.low(stage, STEPS - 1), 8)
-        for f in range(FIELDS):
-            for row in range(rows + 2):
-                if f < MOVING or 0 < row <= rows:
-                    out_state[f, row, at] = even[STEPS // 2, f, STEPS - 1 + row, at]
-        for f in range(MOVING):
-            for group in range(GROUPS):
-                out_near[f, group, at] = even_near[STEPS // 2, f, group, at]
-
-    pl.semaphore_wait(barrier, 3 + has_below.astype(jnp.int32) + has_above.astype(jnp.int32))
+    pl.semaphore_wait(barrier, 5 + has_below.astype(jnp.int32) + has_above.astype(jnp.int32))
 
     @pl.when(has_below)
     def _():
@@ -562,6 +608,7 @@
         return carry
 
     lax.fori_loop(0, own_chunks, fill_own, 0)
+    lax.fori_loop(0, own_chunks, send_across, 0)
     tail = pl.ds((planes - lead) * rows, lead * rows)
     lab_up[0 : lead * rows] = lab[tail]
     for i in range(2):
@@ -590,37 +637,39 @@
 
         lax.fori_loop(0, 8 * pieces - lead - 1, melt_plane, 0)
 
+    def z_body(chunk, carry):
+        send_z(chunk)
+        return carry
+
+    def pass_on(stage):
+        @pl.when(stage == 0)
+        def _():
+            take(pieces)
+
+        @pl.when(stage == 1)
+        def _():
+            lax.fori_loop(own_chunks + 1, chunks, z_body, 0)
+
     def beat(it, carry):
-        first_z = jnp.where(it > own_chunks, it - 1, it)
-        last_z = jnp.where(it == own_chunks, it, jnp.where(it == own_chunks + 2, chunks, jnp.where(it > own_chunks + 2, first_z, first_z + 1)))
-
-        def z_body(chunk, carry):
-            send_z(chunk)
-            return carry
-
-        @pl.when((it > own_chunks) & (it == 2 * (pieces - 1)))
+        lax.fori_loop(jnp.where(it == 3, 2, it), jnp.where(it == 3, 4, jnp.where(it < 2, it + 1, it)), z_body, 0)
+
+        @pl.when((it == 0) | ((it >= 2) & (it < pieces)))
         def _():
             take(it)
 
-        lax.fori_loop(first_z, last_z, z_body, 0)
-
-        @pl.when((it < 2 * (pieces - 1)) & (lax.rem(it, 2) == 0))
-        def _():
-            take(it)
+        @pl.when(it >= 1)
+        def _():
+            receive_z(it - 1)
+            unpack(it - 1)
 
         @pl.when(it >= 2)
         def _():
-            either(it - 2, lambda k: z_copy(k).wait_recv())
-            unpack(it - 2)
-
-        @pl.when(it >= 3)
-        def _():
-            compute(it - 3)
+            compute(it - 2)
 
         return carry
 
     def take(it):
-        piece = lax.div(it, 2)
+        piece = jnp.maximum(it - 1, 0)
         for k in range(pieces):
             @pl.when(has_above & (piece == k))
             def _():
@@ -630,15 +679,23 @@
         fill(lab_up, pot_up, 8 * piece, 8 * (own_chunks + piece))
         send_y(own_chunks + piece)
 
-    lax.fori_loop(0, plan.stages + 3, beat, 0)
+    lax.fori_loop(0, plan.stages + 2, beat, 0)
 
     def drain(chunk, carry):
-        def wait(k):
-            for copy in y_copies(k):
+        def wait(copies):
+            for copy in copies:
                 copy.wait_send()
-            z_copy(k).wait_send()
-
-        either(chunk, wait)
+
+        either(chunk, lambda k: wait(y_copies(k)))
+
+        @pl.when(chunk >= own_chunks)
+        def _():
+            z_copy(chunk).wait_send()
+
+        @pl.when(chunk < own_chunks)
+        def _():
+            either(chunk, lambda k: wait(across_copies(k)))
+
         return carry
 
     lax.fori_loop(0, chunks, drain, 0)
@@ -664,10 +721,11 @@
 
     def body(tile, carry):
         low = begin + 8 * tile
-        for row in range(1, rows + 1):
-            sums = main_sums(state, row, low, side_sums(state, near, row, low, at_left, at_right, STEPS - 1))
-            p, m = last_step(sums, *center(state, row, low))
-            at = pl.ds(8 * tile * rows + row - 1, 8, stride=rows)
+        for row in range(rows):
+            src = state.at[0]
+            sums = main_sums(src, STEPS + row, low, side_sums(src, near.at[0], STEPS + row, low, at_left, at_right))
+            p, m = last_step(sums, *center(src, STEPS + row, low))
+            at = pl.ds(8 * tile * rows + row, 8, stride=rows)
             for f in range(4):
                 p_out[f, at, :] = p[f]
             for i in range(2):
@@ -692,14 +750,14 @@
     f32 = jnp.float32
     dma = pltpu.SemaphoreType.DMA
     deep, tall, chunks = plan.deep, plan.tall, plan.chunks
-    evens, odds = STEPS // 2 + 1, STEPS // 2
+    evens, odds = STEPS // 2, STEPS // 2
     upper = 8 * plan.pieces * rows
-    kept = (FIELDS * (rows + 2) + MOVING * GROUPS) * deep * width * 4
+    kept = (FIELDS * tall + MOVING * GROUPS) * deep * width * 4
     state, near = pl.pallas_call(
         functools.partial(front_kernel, plan, mesh_shape, levels),
         out_shape=(
-            pltpu.VMEM((FIELDS, rows + 2, deep, width), f32),
-            pltpu.VMEM((MOVING, GROUPS, deep, width), f32),
+            pltpu.VMEM((1, FIELDS, tall, deep, width), f32),
+            pltpu.VMEM((1, MOVING, GROUPS, deep, width), f32),
         ),
         in_specs=[hbm, hbm, hbm, hbm],
         out_specs=(vmem, vmem),
@@ -713,16 +771,20 @@
             pltpu.VMEM((3, tall, deep, width), f32),
             pltpu.VMEM((3, GROUPS, deep, width), f32),
             pltpu.VMEM((3, GROUPS, deep, width), f32),
+            pltpu.VMEM((3, GROUPS, 8 * plan.own_chunks, width), f32),
+            pltpu.VMEM((3, 3, GROUPS, 8 * plan.own_chunks, width), f32),
             pltpu.VMEM((evens, FIELDS, tall, deep, width), f32),
             pltpu.VMEM((odds, FIELDS, tall, deep, width), f32),
             pltpu.VMEM((evens, MOVING, GROUPS, deep, width), f32),
             pltpu.VMEM((odds, MOVING, GROUPS, deep, width), f32),
             pltpu.VMEM((evens, FIELDS, GROUPS, deep, width), f32),
             pltpu.VMEM((odds, FIELDS, GROUPS, deep, width), f32),
+            pltpu.VMEM((1, FIELDS, GROUPS, deep, width), f32),
             pltpu.VMEM((BATCH, MOVING, 8, width), f32),
             pltpu.VMEM((MOVING, GROUPS, 8, width), f32),
             dma((4,)), dma((3 * chunks,)), dma((3 * chunks,)),
             dma((2 * chunks,)), dma((2 * chunks,)), dma((chunks,)), dma((chunks,)),
+            dma((3 * plan.own_chunks,)), dma((3 * plan.own_chunks,)),
         ],
         compiler_params=pltpu.CompilerParams(collective_id=0, has_side_effects=True, vmem_limit_bytes=(VMEM_BYTES - kept) // 4096 * 4096),
         name="front",

time: 27.3 us -> 26.9 us (0.985)
  Pallas kernels: 26.4 us -> 26.1 us
    pallas_call x1, Pallas kernels: 24.7 us -> 24.4 us  [on_device(): pl.pallas_call(functools.partial(front_kernel, plan, mesh_shape, levels),...]
where the time goes in v6:
time: 26.9 us; the launch traced here: 26.7 us
  Pallas kernels  26.1 us (97%)
  between operations  0.64 us (2%)
    pallas_call x1, Pallas kernels, on_device(): pl.pallas_call(functools.partial(front_kernel, plan, mesh_shape, levels),...  24.4 us
    pallas_call x1, Pallas kernels, on_device(): pl.pallas_call(functools.partial(last_kernel, plan), out_shape=(jax.Shape...  1.69 us

profile of v6, /device:TPU:0, one launch (start us, length us, event | category | flops | bytes accessed | tf_op | source)
XLA Modules:
  0.0 26.7 jit_solution(8600166531036955406)
XLA Ops:
  0.6 24.4 %front.1 = (f32[1,11,18,48,128]{4,3,2,1,0:T(8,128)S(1)}, f32[1,5,3,48,128]{4,3,2,1,0:T(8,128)S(1)}) custom-call(s32[256,128]{1,0:T(8,128)} %bitcast.6, f32[2,256,128]{2,1,0:T(8,128)} %bitcast.5, s32[128,128]{1,0:T(8,128)} %bitcast.7, f32[2,8]{1,0:T(2,128)} %table_hbm.1), custom_call_target="tpu_custom_call" | custom-call | tf_op jit(solution)/shard_map/front/pallas_call | solution.py:756
  25.1 1.7 %last.1 = (f32[4,256,128]{2,1,0:T(8,128)}, f32[2,256,128]{2,1,0:T(8,128)}) custom-call(f32[1,11,18,48,128]{4,3,2,1,0:T(8,128)S(1)} %get-tuple-element.6.state, f32[1,5,3,48,128]{4,3,2,1,0:T(8,128)S(1)} %get-tuple-element.7.near), custom_call_target="tpu_custom_call" | custom-call | tf_op jit(solution)/shard_map/last/pallas_call | solution.py:793

commit v7 on v6

--- a/solution.py
+++ b/solution.py
@@ -14,6 +14,7 @@
 SLOT = 2 * HALF
 GROUPS = 3
 LAG = 5
+HOOK = 2
 BATCH = 8
 FIELDS = 11
 MOVING = 5
@@ -559,37 +560,48 @@
         top = stage_of(top_plane, STEPS_BEFORE)
         below_melt = (stage <= top) | jnp.logical_not(is_last)
 
-        for step in range(1, STEPS):
-            state, near, strips, slot = buffers(step)
-            out = (state, strips, near, slot)
-
-            if step <= STEPS_BEFORE:
-                pl.when(below_melt)(functools.partial(row_steps, stage, step))
-            else:
+        eventful = (is_first & (stage == stage_of(first_plane, STEPS_BEFORE))) | (is_last & (stage >= top))
+
+        @pl.when(jnp.logical_not(eventful))
+        def _():
+            for step in range(1, STEPS):
                 row_steps(stage, step)
-
-            if step < STEPS_BEFORE:
-                @pl.when(is_last & (stage == stage_of(top_plane, step)))
-                def _():
-                    copy_plane(*out, top_plane - 1, top_plane)
-            else:
-                @pl.when(is_first & (stage == stage_of(first_plane, step)))
-                def _():
-                    copy_plane(*out, first_plane, first_plane - 1)
-
-            if step == 2:
-                pass_on(stage)
-
-            if step == STEPS_BEFORE:
-                @pl.when(is_last & (stage >= top))
-                def _():
-                    melt_fill(stage)
-                    begin(stage, step + 1)
-
-            if step == STEPS - 1:
-                @pl.when(is_last & (stage == stage_of(last_plane, step)))
-                def _():
-                    copy_plane(*out, last_plane, last_plane + 1)
+                if step == HOOK:
+                    pass_on(stage)
+
+        @pl.when(eventful)
+        def _():
+            for step in range(1, STEPS):
+                state, near, strips, slot = buffers(step)
+                out = (state, strips, near, slot)
+
+                if step <= STEPS_BEFORE:
+                    pl.when(below_melt)(functools.partial(row_steps, stage, step))
+                else:
+                    row_steps(stage, step)
+
+                if step < STEPS_BEFORE:
+                    @pl.when(is_last & (stage == stage_of(top_plane, step)))
+                    def _():
+                        copy_plane(*out, top_plane - 1, top_plane)
+                else:
+                    @pl.when(is_first & (stage == stage_of(first_plane, step)))
+                    def _():
+                        copy_plane(*out, first_plane, first_plane - 1)
+
+                if step == HOOK:
+                    pass_on(stage)
+
+                if step == STEPS_BEFORE:
+                    @pl.when(is_last & (stage >= top))
+                    def _():
+                        melt_fill(stage)
+                        begin(stage, step + 1)
+
+                if step == STEPS - 1:
+                    @pl.when(is_last & (stage == stage_of(last_plane, step)))
+                    def _():
+                        copy_plane(*out, last_plane, last_plane + 1)
 
     pl.semaphore_wait(barrier, 5 + has_below.astype(jnp.int32) + has_above.astype(jnp.int32))
 

time: 26.9 us -> 25.9 us (0.963)
  Pallas kernels: 26.1 us -> 25.2 us
    pallas_call x1, Pallas kernels: 24.4 us -> 23.5 us  [on_device(): pl.pallas_call(functools.partial(front_kernel, plan, mesh_shape, levels),...]
where the time goes in v7:
time: 25.9 us; the launch traced here: 25.8 us
  Pallas kernels  25.2 us (97%)
  between operations  0.64 us (2%)
    pallas_call x1, Pallas kernels, on_device(): pl.pallas_call(functools.partial(front_kernel, plan, mesh_shape, levels),...  23.5 us
    pallas_call x1, Pallas kernels, on_device(): pl.pallas_call(functools.partial(last_kernel, plan), out_shape=(jax.Shape...  1.69 us

profile of v7, /device:TPU:0, one launch (start us, length us, event | category | flops | bytes accessed | tf_op | source)
XLA Modules:
  0.0 25.8 jit_solution(7150977326361297793)
XLA Ops:
  0.6 23.5 %front.1 = (f32[1,11,18,48,128]{4,3,2,1,0:T(8,128)S(1)}, f32[1,5,3,48,128]{4,3,2,1,0:T(8,128)S(1)}) custom-call(s32[256,128]{1,0:T(8,128)} %bitcast.6, f32[2,256,128]{2,1,0:T(8,128)} %bitcast.5, s32[128,128]{1,0:T(8,128)} %bitcast.7, f32[2,8]{1,0:T(2,128)} %table_hbm.1), custom_call_target="tpu_custom_call" | custom-call | tf_op jit(solution)/shard_map/front/pallas_call | solution.py:768
  24.1 1.7 %last.1 = (f32[4,256,128]{2,1,0:T(8,128)}, f32[2,256,128]{2,1,0:T(8,128)}) custom-call(f32[1,11,18,48,128]{4,3,2,1,0:T(8,128)S(1)} %get-tuple-element.6.state, f32[1,5,3,48,128]{4,3,2,1,0:T(8,128)S(1)} %get-tuple-element.7.near), custom_call_target="tpu_custom_call" | custom-call | tf_op jit(solution)/shard_map/last/pallas_call | solution.py:805

commit v8 on v7

--- a/solution.py
+++ b/solution.py
@@ -562,12 +562,17 @@
 
         eventful = (is_first & (stage == stage_of(first_plane, STEPS_BEFORE))) | (is_last & (stage >= top))
 
-        @pl.when(jnp.logical_not(eventful))
+        @pl.when(jnp.logical_not(eventful) & (stage < 2))
         def _():
             for step in range(1, STEPS):
                 row_steps(stage, step)
                 if step == HOOK:
                     pass_on(stage)
+
+        @pl.when(jnp.logical_not(eventful) & (stage >= 2))
+        def _():
+            for step in range(1, STEPS):
+                row_steps(stage, step)
 
         @pl.when(eventful)
         def _():

time: 25.9 us -> 25.7 us (level)
  Pallas kernels: 25.2 us -> 24.9 us
    pallas_call x1, Pallas kernels: 23.5 us -> 23.2 us  [on_device(): pl.pallas_call(functools.partial(front_kernel, plan, mesh_shape, levels),...]
where the time goes in v8:
time: 25.7 us; the launch traced here: 25.5 us
  Pallas kernels  24.9 us (97%)
  between operations  0.64 us (2%)
    pallas_call x1, Pallas kernels, on_device(): pl.pallas_call(functools.partial(front_kernel, plan, mesh_shape, levels),...  23.2 us
    pallas_call x1, Pallas kernels, on_device(): pl.pallas_call(functools.partial(last_kernel, plan), out_shape=(jax.Shape...  1.69 us

profile of v8, /device:TPU:0, one launch (start us, length us, event | category | flops | bytes accessed | tf_op | source)
XLA Modules:
  0.0 25.5 jit_solution(4424256076668287261)
XLA Ops:
  0.6 23.2 %front.1 = (f32[1,11,18,48,128]{4,3,2,1,0:T(8,128)S(1)}, f32[1,5,3,48,128]{4,3,2,1,0:T(8,128)S(1)}) custom-call(s32[256,128]{1,0:T(8,128)} %bitcast.6, f32[2,256,128]{2,1,0:T(8,128)} %bitcast.5, s32[128,128]{1,0:T(8,128)} %bitcast.7, f32[2,8]{1,0:T(2,128)} %table_hbm.1), custom_call_target="tpu_custom_call" | custom-call | tf_op jit(solution)/shard_map/front/pallas_call | solution.py:773
  23.8 1.7 %last.1 = (f32[4,256,128]{2,1,0:T(8,128)}, f32[2,256,128]{2,1,0:T(8,128)}) custom-call(f32[1,11,18,48,128]{4,3,2,1,0:T(8,128)S(1)} %get-tuple-element.6.state, f32[1,5,3,48,128]{4,3,2,1,0:T(8,128)S(1)} %get-tuple-element.7.near), custom_call_target="tpu_custom_call" | custom-call | tf_op jit(solution)/shard_map/last/pallas_call | solution.py:810

commit v9 on v8

--- a/solution.py
+++ b/solution.py
@@ -622,10 +622,9 @@
     def fill_own(chunk, carry):
         fill(lab, pot, plan.base + 8 * chunk, 8 * chunk)
         either(chunk, send_y)
-        return carry
+        return send_across(chunk, carry)
 
     lax.fori_loop(0, own_chunks, fill_own, 0)
-    lax.fori_loop(0, own_chunks, send_across, 0)
     tail = pl.ds((planes - lead) * rows, lead * rows)
     lab_up[0 : lead * rows] = lab[tail]
     for i in range(2):

time: 25.7 us -> 25.7 us (level)
  no operation moved by 1% of the time
where the time goes in v9:
time: 25.7 us; the launch traced here: 25.5 us
  Pallas kernels  24.9 us (97%)
  between operations  0.64 us (2%)
    pallas_call x1, Pallas kernels, on_device(): pl.pallas_call(functools.partial(front_kernel, plan, mesh_shape, levels),...  23.2 us
    pallas_call x1, Pallas kernels, on_device(): pl.pallas_call(functools.partial(last_kernel, plan), out_shape=(jax.Shape...  1.69 us

profile of v9, /device:TPU:0, one launch (start us, length us, event | category | flops | bytes accessed | tf_op | source)
XLA Modules:
  0.0 25.5 jit_solution(2585115756690291738)
XLA Ops:
  0.6 23.2 %front.1 = (f32[1,11,18,48,128]{4,3,2,1,0:T(8,128)S(1)}, f32[1,5,3,48,128]{4,3,2,1,0:T(8,128)S(1)}) custom-call(s32[256,128]{1,0:T(8,128)} %bitcast.6, f32[2,256,128]{2,1,0:T(8,128)} %bitcast.5, s32[128,128]{1,0:T(8,128)} %bitcast.7, f32[2,8]{1,0:T(2,128)} %table_hbm.1), custom_call_target="tpu_custom_call" | custom-call | tf_op jit(solution)/shard_map/front/pallas_call | solution.py:772
  23.8 1.7 %last.1 = (f32[4,256,128]{2,1,0:T(8,128)}, f32[2,256,128]{2,1,0:T(8,128)}) custom-call(f32[1,11,18,48,128]{4,3,2,1,0:T(8,128)S(1)} %get-tuple-element.6.state, f32[1,5,3,48,128]{4,3,2,1,0:T(8,128)S(1)} %get-tuple-element.7.near), custom_call_target="tpu_custom_call" | custom-call | tf_op jit(solution)/shard_map/last/pallas_call | solution.py:809
